TPU v7x, 512 devices: a whole 4x8x8 slice. The times are simulated.
512 devices in a mesh: wave: 32 (over x, y), freq: 16 (over z, core).
Axes of the slice: x: 4, y: 8, z: 8, core: 2. Of those that a mesh axis runs over, the one named last changes fastest.
Arguments:
- res_re: float32 [8192, 8192], P('wave', 'freq'), may hold values from -6 to 6
- res_im: float32 [8192, 8192], P('wave', 'freq'), may hold values from -6 to 6
- basis_re: float32 [256, 8192], P(None, 'freq'), may hold values from -0.046875 to 0.046875
- basis_im: float32 [256, 8192], P(None, 'freq'), may hold values from -0.046875 to 0.046875
- lengths: int32 [8192], P('wave'), may hold values from 8 to 64
- pivots: int32 [128], replicated, may hold values from 0 to 8191, as said below
Outputs:
- coef_re: float32 [8192, 128], P('wave')
- coef_im: float32 [8192, 128], P('wave')
- new_re: float32 [8192, 8192], P('wave', 'freq')
- new_im: float32 [8192, 8192], P('wave', 'freq')
- errors: float32 [8192], P('wave')
Inputs may be any that keep to these rules, and one draw needn't show every extreme that they name: The 128 pivots are distinct waveform indices.
All inputs are finite; a program needn't handle non-finite values. Where the computation divides by a largest or mean magnitude, that divisor is 1e-20 or more.
Results may differ from a plain program's by a relative error of at most 0.0003.
Values sent between devices are 32-bit elements; how exact they have to be, the bound alone decides.
A program may use at most 64 MiB of HBM per device.

v0:
```python
import jax
import jax.numpy as jnp
from jax import lax
from jax.sharding import Mesh
from jax.sharding import PartitionSpec as P

BIN_BLOCK = 128
NS_STEPS = 6
FREQ = ("freq_0", "freq_1")


epsilon = 1e-06


def cut_along(shard, dim, peers):
    before, after = (shard.shape[:dim], shard.shape[dim + 1 :])
    return jnp.moveaxis(shard.reshape(*before, peers, -1, *after), dim, 0)


def sum_at_owner(shard, axis, dim):
    peers = lax.axis_size(axis)
    blocks = lax.all_to_all(cut_along(shard, dim, peers), axis, 0, 0, tiled=True)
    return jnp.sum(blocks, axis=0)


def in_one_piece(arrays, axis, dim, along):
    ends, at = ([], 0)
    for a in arrays[:-1]:
        at += a.shape[along]
        ends.append(at)
    both = jnp.concatenate(arrays, axis=along)
    return tuple(jnp.split(sum_at_owner(both, axis, dim), ends, axis=along))


def filled_up(lines, peers):
    spare = -lines.shape[0] % peers
    if not spare:
        return lines
    return jnp.concatenate([lines, jnp.zeros((spare, *lines.shape[1:]), lines.dtype)])


def copy_for_each(shard, axis):
    peers = lax.axis_size(axis)
    return lax.all_to_all(
        jnp.broadcast_to(shard[None], (peers, *shard.shape)), axis, 0, 0, tiled=True
    )


def joined_along(blocks, dim):
    shape = list(blocks.shape[1:])
    shape[dim] *= blocks.shape[0]
    return jnp.moveaxis(blocks, 0, dim).reshape(shape)


def gathered_by_axis(shard, axes, dim):
    far, near = axes
    blocks = copy_for_each(copy_for_each(shard, far), near)
    return joined_along(blocks.swapaxes(0, 1).reshape(-1, *shard.shape), dim)


def sum_in_two_steps(shard, axes, dim):
    far, near = axes
    blocks = cut_along(shard, dim, lax.axis_size(far))
    nearer = sum_at_owner(blocks, near, dim + 1)
    arrived = lax.all_to_all(nearer, far, split_axis=0, concat_axis=0, tiled=True)
    return arrived.sum(axis=0)


def nested_sum(shard, axes):
    padded = filled_up(shard, lax.axis_size(axes[0]) * lax.axis_size(axes[1]))
    whole = gathered_by_axis(sum_in_two_steps(padded, axes, 0), axes, 0)
    return lax.slice_in_dim(whole, 0, len(shard)).reshape(shard.shape)


def together(arrays, axis):
    ravelled, at, finished = (jnp.concatenate([a.reshape(-1) for a in arrays]), 0, [])
    subtotal = nested_sum(ravelled, axis)
    for a in arrays:
        finished.append(subtotal[at : at + a.size].reshape(a.shape))
        at += a.size
    return tuple(finished)


def sent_together(arrays, axis, dim, along):
    ends, at = ([], 0)
    for a in arrays[:-1]:
        at += a.shape[along]
        ends.append(at)
    both = jnp.concatenate(arrays, axis=along)
    return tuple(jnp.split(lax.all_gather(both, axis, axis=dim, tiled=True), ends, axis=along))


def gathered_copies(shard, axis, dim):
    blocks = copy_for_each(shard, axis)
    return joined_along(blocks, dim)


def total_of(shard, axes):
    own = sum_at_owner(filled_up(shard, lax.axis_size(axes)), axes, 0)
    whole = gathered_copies(own, axes, 0)
    return whole[: len(shard)].reshape(shard.shape)


def packed_total(arrays, axis):
    ravelled, at, finished = (jnp.concatenate([a.reshape(-1) for a in arrays]), 0, [])
    subtotal = total_of(ravelled, axis)
    for a in arrays:
        finished.append(subtotal[at : at + a.size].reshape(a.shape))
        at += a.size
    return tuple(finished)


def taken_together(shard, axis):
    return copy_for_each(shard, axis).sum(axis=0)


def plain(left, right):
    return jnp.dot(left, right, precision=lax.Precision.HIGHEST, preferred_element_type=jnp.float32)


def against(left, right):
    return lax.dot_general(
        left,
        right,
        (((1,), (1,)), ((), ())),
        precision=lax.Precision.HIGHEST,
        preferred_element_type=jnp.float32,
    )


def product(left_re, left_im, right_re, right_im):
    return (
        plain(left_re, right_re) - plain(left_im, right_im),
        plain(left_re, right_im) + plain(left_im, right_re),
    )


def inner(left_re, left_im, right_re, right_im):
    return (
        against(left_re, right_re) + against(left_im, right_im),
        against(left_im, right_re) - against(left_re, right_im),
    )


def whiten(gram_re, gram_im, pivot_re, pivot_im):
    scale = 1.0 / jnp.sqrt(jnp.diagonal(gram_re) + epsilon)
    outer = scale[:, None] * scale[None, :]
    gram_re = gram_re * outer
    gram_im = gram_im * outer
    unit_re = pivot_re * scale[:, None]
    unit_im = pivot_im * scale[:, None]
    bound = jnp.max(jnp.sum(jnp.abs(gram_re) + jnp.abs(gram_im), axis=1))
    ident = jnp.eye(gram_re.shape[0], dtype=jnp.float32)
    your_re = gram_re / bound
    your_im = gram_im / bound
    zed_re = ident
    zed_im = jnp.zeros_like(ident)
    for step in range(NS_STEPS):
        mix_re, mix_im = product(zed_re, zed_im, your_re, your_im)
        step_re = 1.5 * ident - 0.5 * mix_re
        step_im = -0.5 * mix_im
        your_re, your_im = product(your_re, your_im, step_re, step_im)
        zed_re, zed_im = product(step_re, step_im, zed_re, zed_im)
    factor = 1.0 / jnp.sqrt(bound)
    return product(zed_re * factor, zed_im * factor, unit_re, unit_im)


def body(res_re, res_im, basis_re, basis_im, lengths, pivots):
    wave_rows = res_re.shape[0]
    freq_cols = res_re.shape[1]
    bins = lax.axis_index(FREQ) * freq_cols + jnp.arange(freq_cols, dtype=jnp.int32)
    mask = (bins[None, :] < BIN_BLOCK * lengths[:, None]).astype(jnp.float32)
    live_re = res_re * mask
    live_im = res_im * mask
    owned = lax.axis_index("wave") * wave_rows + jnp.arange(wave_rows, dtype=jnp.int32)
    select = (pivots[:, None] == owned[None, :]).astype(jnp.float32)
    picked_re = plain(select, live_re)
    picked_im = plain(select, live_im)
    pivot_re, pivot_im = in_one_piece((picked_re, picked_im), "wave", 0, 1)
    cross_re, cross_im = inner(pivot_re, pivot_im, basis_re, basis_im)
    basis_gram_re, basis_gram_im = inner(basis_re, basis_im, basis_re, basis_im)
    cross_re, cross_im, basis_gram_re, basis_gram_im = together(
        (cross_re, cross_im, basis_gram_re, basis_gram_im), ("freq_0", "freq_1")
    )
    twist_re, twist_im = product(cross_re, cross_im, basis_gram_re, basis_gram_im)
    total_re = 2.0 * cross_re - twist_re
    total_im = 2.0 * cross_im - twist_im
    back_re, back_im = product(total_re, total_im, basis_re, basis_im)
    pivot_re = pivot_re - back_re
    pivot_im = pivot_im - back_im
    pivot_re, pivot_im = sent_together((pivot_re, pivot_im), "wave", 0, 1)
    gram_re, gram_im = inner(pivot_re, pivot_im, pivot_re, pivot_im)
    gram_re, gram_im = packed_total((gram_re, gram_im), FREQ)
    block_re, block_im = whiten(gram_re, gram_im, pivot_re, pivot_im)
    coef_re, coef_im = inner(live_re, live_im, block_re, block_im)
    coef_re, coef_im = packed_total((coef_re, coef_im), FREQ)
    back_re, back_im = product(coef_re, coef_im, block_re, block_im)
    new_re = (live_re - back_re) * mask
    new_im = (live_im - back_im) * mask
    partial_sq = jnp.sum(new_re * new_re + new_im * new_im, axis=1)
    summed_sq = taken_together(partial_sq, FREQ)
    errors = summed_sq / (BIN_BLOCK * lengths).astype(jnp.float32)
    return (coef_re, coef_im, new_re, new_im, errors)


def solution(mesh):
    torus = Mesh(mesh.devices.reshape(mesh.shape["wave"], 8, 2), ("wave", "freq_0", "freq_1"))
    in_specs = (P("wave", FREQ), P("wave", FREQ), P(None, FREQ), P(None, FREQ), P("wave"), P())
    out_specs = (P("wave", None), P("wave", None), P("wave", FREQ), P("wave", FREQ), P("wave"))
    return jax.shard_map(body, mesh=torus, in_specs=in_specs, out_specs=out_specs, check_vma=False)
```

profile of v0, /device:TPU:1, one launch (start us, length us, event | category | flops | bytes accessed | tf_op | source)
XLA Modules:
  0.0 229.3 jit_solution(18279530365981054821)
XLA Ops:
  0.7 0.8 iota_add_fusion.1
  1.4 1.5 fusion.35
  3.5 0.9 reshape.132
  4.4 10.6 %all-to-all-start = ((f32[32,4,1024]{2,1,0:T(4,128)}), f32[32,4,1024]{2,1,0:T(4,128)S(1)}, u32[]{:S(2)}, u32[]{:S(2)}) async-start(f32[32,4,1024]{2,1,0:T(4,128)} %reshape.132), calls=%async_computation | async-start | bytes 1048576 | tf_op jit(solution)/shard_map/all_to_all | solution.py:22
  15.1 0.6 fusion.123
  15.7 0.6 fusion.4
  16.4 0.6 fusion.122
  17.1 0.6 fusion.5
  17.8 11.7 %all-to-all-done = f32[32,4,1024]{2,1,0:T(4,128)S(1)} async-done(((f32[32,4,1024]{2,1,0:T(4,128)}), f32[32,4,1024]{2,1,0:T(4,128)S(1)}, u32[]{:S(2)}, u32[]{:S(2)}) %all-to-all-start) | async-done | bytes 524320 | tf_op jit(solution)/shard_map/all_to_all | solution.py:22
  29.7 0.5 fusion.94
  30.2 0.5 fusion.98
  30.7 0.5 fusion.30
  31.3 0.5 fusion.31
  32.2 6.9 %all_to_all.66 = f32[2,8,8320]{2,1,0:T(8,128)S(1)} all-to-all(f32[2,8,8320]{2,1,0:T(8,128)S(1)} %copy.16), channel_id=1, replica_groups=mesh['wave'=32,'freq_0'=8,'freq_1'=2] {'freq_1'}, dimensions={0} | all-to-all | bytes 1064960 | tf_op jit(solution)/shard_map/all_to_all | solution.py:22
  39.3 21.1 %all_to_all.67 = f32[8,1,8320]{2,1,0:T(1,128)S(1)} all-to-all(f32[8,1,8320]{2,1,0:T(1,128)S(1)} %all_to_all.45), channel_id=1, replica_groups=mesh['wave'=32,'freq_0'=8,'freq_1'=2] {'freq_0'}, dimensions={0} | all-to-all | bytes 532480 | tf_op jit(solution)/shard_map/all_to_all | solution.py:65
  60.7 12.2 %all_to_all.68 = f32[8,1,8320]{2,1,0:T(1,128)S(1)} all-to-all(f32[8,1,8320]{2,1,0:T(1,128)S(1)} %broadcast_in_dim.14), channel_id=1, replica_groups=mesh['wave'=32,'freq_0'=8,'freq_1'=2] {'freq_0'}, dimensions={0} | all-to-all | bytes 532480 | tf_op jit(solution)/shard_map/all_to_all | solution.py:44
  73.0 6.9 %all_to_all.69 = f32[2,8,8320]{2,1,0:T(8,128)S(1)} all-to-all(f32[2,8,8320]{2,1,0:T(8,128)S(1)} %broadcast_in_dim.16), channel_id=1, replica_groups=mesh['wave'=32,'freq_0'=8,'freq_1'=2] {'freq_1'}, dimensions={0} | all-to-all | bytes 1064960 | tf_op jit(solution)/shard_map/all_to_all | solution.py:44
  83.0 37.0 %all-gather = f32[32,4,1024]{2,1,0:T(4,128)S(1)} all-gather(f32[1,4,1024]{2,1,0:T(4,128)S(1)} %maximum_bitcast_fusion), channel_id=1, replica_groups=mesh['wave'=32,'freq_0'=8,'freq_1'=2] {'wave'}, dimensions={0}, use_global_device_ids=true | all-gather | bytes 540672 | tf_op jit(solution)/shard_map/all_gather | solution.py:90
  121.9 24.1 %all_to_all.70 = f32[16,1,2048]{2,1,0:T(1,128)S(1)} all-to-all(f32[16,1,2048]{2,1,0:T(1,128)S(1)} %all_to_all.49), channel_id=1, replica_groups=mesh['wave'=32,'freq_0'=8,'freq_1'=2] {'freq_0','freq_1'}, dimensions={0} | all-to-all | bytes 262144 | tf_op jit(solution)/shard_map/all_to_all | solution.py:22
  146.1 0.7 broadcast_in_dim.17
  146.8 3.4 %all-to-all-start.6 = ((f32[16,1,2048]{2,1,0:T(1,128)}), f32[16,1,2048]{2,1,0:T(1,128)S(1)}, u32[]{:S(2)}, u32[]{:S(2)}) async-start(f32[16,1,2048]{2,1,0:T(1,128)} %broadcast_in_dim.17), calls=%async_computation.6 | async-start | bytes 262144 | tf_op jit(solution)/shard_map/all_to_all | solution.py:44
  150.2 8.4 %all-to-all-done.6 = f32[16,1,2048]{2,1,0:T(1,128)S(1)} async-done(((f32[16,1,2048]{2,1,0:T(1,128)}), f32[16,1,2048]{2,1,0:T(1,128)S(1)}, u32[]{:S(2)}, u32[]{:S(2)}) %all-to-all-start.6) | async-done | bytes 131104 | tf_op jit(solution)/shard_map/all_to_all | solution.py:44
  158.7 1.2 gather_fusion
  160.1 0.6 reduce_max.9
  161.4 0.7 multiply_reduce_fusion
  162.2 0.9 fusion.25
  163.3 0.9 fusion.117
  164.4 0.9 fusion.23
  165.3 0.9 fusion.115
  166.4 0.9 convolution_subtract_fusion.18
  167.3 0.9 convolution_add_fusion.18
  180.1 0.5 fusion.60
  180.5 0.5 fusion.64
  181.2 0.5 convolution_subtract_fusion.1
  182.0 0.6 fusion.34
  182.7 0.6 fusion.32
  183.3 0.5 convolution_add_fusion.1
  183.8 0.6 convolution_subtract_fusion.3
  184.4 0.6 convolution_add_fusion.3
  185.4 14.3 %all_to_all.71 = f32[16,1,4096]{2,1,0:T(1,128)S(1)} all-to-all(f32[16,1,4096]{2,1,0:T(1,128)S(1)} %all_to_all.52), channel_id=1, replica_groups=mesh['wave'=32,'freq_0'=8,'freq_1'=2] {'freq_0','freq_1'}, dimensions={0} | all-to-all | bytes 524288 | tf_op jit(solution)/shard_map/all_to_all | solution.py:22
  200.1 14.3 %all_to_all.72 = f32[16,1,4096]{2,1,0:T(1,128)S(1)} all-to-all(f32[16,1,4096]{2,1,0:T(1,128)S(1)} %broadcast_in_dim.18), channel_id=1, replica_groups=mesh['wave'=32,'freq_0'=8,'freq_1'=2] {'freq_0','freq_1'}, dimensions={0} | all-to-all | bytes 524288 | tf_op jit(solution)/shard_map/all_to_all | solution.py:44
  214.5 0.6 fusion.155
  215.1 0.6 fusion.154
  215.7 0.7 fusion.3
  216.4 1.5 add_reduce_fusion
  217.9 10.1 %all_to_all.73 = f32[16,1,256]{2,1,0:T(1,128)S(1)} all-to-all(f32[16,1,256]{2,1,0:T(1,128)S(1)} %broadcast_in_dim.21), channel_id=1, replica_groups=mesh['wave'=32,'freq_0'=8,'freq_1'=2] {'freq_0','freq_1'}, dimensions={0} | all-to-all | bytes 32768 | tf_op jit(solution)/shard_map/all_to_all | solution.py:44
  228.0 0.6 copy-done.7
  228.7 0.6 convert_divide_fusion
  (128 shorter events, 20.4 us)
Async XLA Ops:
  0.6 14.4 %copy-start = (f32[256,512]{1,0:T(8,128)S(1)}, f32[256,512]{1,0:T(8,128)}, u32[]{:S(2)}) copy-start(f32[256,512]{1,0:T(8,128)} %param.8) | copy-start | bytes 1572868
  0.6 2.3 %copy-start.3 = (f32[256,512]{1,0:T(8,128)S(1)}, f32[256,512]{1,0:T(8,128)}, u32[]{:S(2)}) copy-start(f32[256,512]{1,0:T(8,128)} %param.6) | copy-start | bytes 1572868
  1.4 1.5 copy-start.8
  4.4 10.6 %copy-start.1 = (f32[256,512]{1,0:T(8,128)S(1)}, f32[256,512]{1,0:T(8,128)}, u32[]{:S(2)}) copy-start(f32[256,512]{1,0:T(8,128)} %param.9) | copy-start | bytes 1572868
  4.4 25.2 %all-to-all-start = ((f32[32,4,1024]{2,1,0:T(4,128)}), f32[32,4,1024]{2,1,0:T(4,128)S(1)}, u32[]{:S(2)}, u32[]{:S(2)}) async-start(f32[32,4,1024]{2,1,0:T(4,128)} %reshape.132), calls=%async_computation | async-start | bytes 1048576 | tf_op jit(solution)/shard_map/all_to_all | solution.py:22
  146.8 11.9 %all-to-all-start.6 = ((f32[16,1,2048]{2,1,0:T(1,128)}), f32[16,1,2048]{2,1,0:T(1,128)S(1)}, u32[]{:S(2)}, u32[]{:S(2)}) async-start(f32[16,1,2048]{2,1,0:T(1,128)} %broadcast_in_dim.17), calls=%async_computation.6 | async-start | bytes 262144 | tf_op jit(solution)/shard_map/all_to_all | solution.py:44
  181.0 1.0 copy-start.2
  214.4 0.7 copy-start.6
  214.4 1.9 copy-start.5
  216.4 1.5 copy-start.4
  228.0 0.7 copy-start.7
where the time goes:
time: 230 us; the launch traced here: 229 us
  blocking collectives  147 us (64%)
  matrix products  35.5 us (15%)
  waiting for transfers between devices  20.2 us (9%)
  starting transfers between devices  14 us (6%)
  local copies, waits for them, and re-layouts  6.59 us (3%)
  other arithmetic  3.62 us (2%)
  between operations  2.37 us (1%)
    all_to_all x3, blocking collectives, sum_at_owner(): lax.all_to_all(cut_along(shard, dim, peers), axis, 0, 0, tiled=True)  45.2 us
    all_to_all x4, blocking collectives, copy_for_each(): lax.all_to_all(jnp.broadcast_to(shard[None], (peers, *shard.shape)), axis...  43.6 us
    all_gather x1, blocking collectives, sent_together(): lax.all_gather(both, axis, axis=dim, tiled=True)  37 us
    dot_general x84, matrix products, plain(): jnp.dot(left, right, precision=lax.Precision.HIGHEST, preferred_element_t...  27 us
    all_to_all x1, blocking collectives, sum_in_two_steps(): lax.all_to_all(nearer, far, split_axis=0, concat_axis=0, tiled=True)  21.1 us
    all_to_all x1, waiting for transfers between devices, sum_at_owner(): lax.all_to_all(cut_along(shard, dim, peers), axis, 0, 0, tiled=True)  11.7 us
    all_to_all x1, starting transfers between devices, sum_at_owner(): lax.all_to_all(cut_along(shard, dim, peers), axis, 0, 0, tiled=True)  10.6 us
    dot_general x16, matrix products, against(): lax.dot_general(left, right, (((1,), (1,)), ((), ())), precision=lax.Prec...  8.51 us
  transfers between devices with their start and end apart: 2, of which 2 were waited for; matrix products, arithmetic and copies ran while one was open for 1% of the time, Pallas kernels for 0%

commit v1 on v0

v1 whole, which is shorter than its diff:
```python
import functools

import jax
import jax.numpy as jnp
from jax import lax
from jax.experimental import pallas as pl
from jax.experimental.pallas import tpu as pltpu
from jax.sharding import Mesh
from jax.sharding import PartitionSpec as P

BIN_BLOCK = 128
NS_STEPS = 6
EPSILON = 1e-06
TORUS = (4, 8, 8, 2)
AXES = ("x", "y", "z", "core")
F32 = jnp.float32
BF16 = jnp.bfloat16


def dot(left, right, dims):
    return lax.dot_general(left, right, (dims, ((), ())), preferred_element_type=F32)


NN = ((1,), (0,))
NT = ((1,), (1,))


def halves(a):
    high = a.astype(BF16)
    return high, (a - high.astype(F32)).astype(BF16)


def thirds(a):
    high = a.astype(BF16)
    rest = a - high.astype(F32)
    mid = rest.astype(BF16)
    return high, mid, (rest - mid.astype(F32)).astype(BF16)


def product(left, right, dims):
    lh, ll = left
    rh, rl = right
    along = dims[1][0]
    return dot(jnp.concatenate([lh, ll, lh], axis=1), jnp.concatenate([rh, rh, rl], axis=along), dims)


def chosen(select, a):
    parts = thirds(a)
    return dot(jnp.concatenate([select] * 3, axis=1), jnp.concatenate(parts, axis=0), NN)


def swapped(a, part, axis):
    n = a.shape[axis]
    return jnp.where(part == 0, pltpu.roll(a, n - 4, axis), pltpu.roll(a, 4, axis))


def short_product(chunk, rights, dims):
    high = chunk.astype(BF16).astype(F32)
    both = jnp.concatenate([high, chunk - high], axis=0).astype(BF16)
    out = []
    for rh, rl in rights:
        a = dot(both, rh, dims)
        b = dot(both, rl, dims)
        out.append((a[:8] + a[8:]) + (b[:8] + b[8:]))
    return out


def kernel(
    torus,
    res_re, res_im, basis_re, basis_im, lens, lens_row, piv,
    coef_re, coef_im, new_re, new_im, err,
    live, base, picked, xr, ysum, yr, kout, kin, pall, wt,
    gpart, gpair, ghalf, gin, gfull, cpart, cpair, chalf, cin, cfull, eout, ein,
    xs_s, xs_r, ys_s, ys_r, k_s, k_r, ay_s, ay_r, ax_s, ax_r,
    p_s, p_r, gz_s, gz_r, gt_s, gt_r, gc_s, gc_r, cz_s, cz_r, ct_s, ct_r, cc_s, cc_r, e_s, e_r,
):
    nx, ny, nz, nc = torus
    x, y, z, c = (lax.axis_index(a) for a in AXES)
    f = z * nc + c
    rows, bins = res_re.shape
    emb = 8 * nx * ny
    nb = basis_re.shape[0]
    xs = [lax.rem(x + d, nx) for d in range(1, nx)]
    ys = [lax.rem(y + d, ny) for d in range(1, ny)]
    zs = [lax.rem(z + d, nz) for d in range(1, nz)]
    fs = [(lax.rem(z + dz, nz), lax.rem(c + dc, nc)) for dz in range(nz) for dc in range(nc) if dz or dc]

    barrier = pltpu.get_barrier_semaphore()
    peers = [(p, y, z, c) for p in xs] + [(x, p, z, c) for p in ys] + [(x, y, p, q) for p, q in fs]
    for peer in peers:
        pl.semaphore_signal(barrier, inc=1, device_id=peer, device_id_type=pl.DeviceIdType.MESH)

    started = []

    def push(src, dst, send, recv, to):
        copy = pltpu.make_async_remote_copy(
            src_ref=src, dst_ref=dst, send_sem=send, recv_sem=recv, device_id=to,
            device_id_type=pl.DeviceIdType.MESH,
        )
        copy.start()
        started.append(copy)
        return copy

    def arrived(copies):
        for copy in copies:
            copy.wait_recv()

    first_bin = f * bins
    for r in range(0, rows, 64):
        part = slice(r, min(r + 64, rows))
        count = part.stop - part.start
        at = first_bin + lax.broadcasted_iota(jnp.int32, (count, bins), 1)
        mask = (at < BIN_BLOCK * lens[part, :]).astype(F32)
        live[part, :bins] = res_re[part, :] * mask
        live[part, bins:] = res_im[part, :] * mask
    own = (x * ny + y) * rows + lax.broadcasted_iota(jnp.int32, (emb, rows), 1)
    select = (piv[...] == own).astype(F32).astype(BF16)
    is_im = lax.rem(lax.broadcasted_iota(jnp.int32, (emb, bins), 0), 8) // 4
    picked[...] = jnp.where(is_im == 0, chosen(select, live[:, :bins]), chosen(select, live[:, bins:]))

    pl.semaphore_wait(barrier, len(peers))

    span = 8 * ny

    def chunk_of(i, size):
        return pl.ds(pl.multiple_of(i * size, size), size)

    copies = [
        push(picked.at[chunk_of(p, span)], xr.at[i], xs_s.at[i], xs_r.at[i], (p, y, z, c)) for i, p in enumerate(xs)
    ]
    for i, ref in enumerate((basis_re, basis_im)):
        high, low = halves(ref[...])
        base[2 * i] = high
        base[2 * i + 1] = low
    arrived(copies)
    total = picked[chunk_of(x, span), :]
    for i in range(nx - 1):
        total = total + xr[i]
    ysum[...] = total
    copies = [
        push(ysum.at[chunk_of(p, 8)], yr.at[i], ys_s.at[i], ys_r.at[i], (x, p, z, c)) for i, p in enumerate(ys)
    ]
    arrived(copies)
    chunk = ysum[chunk_of(y, 8), :]
    for i in range(ny - 1):
        chunk = chunk + yr[i]

    b_re = (base[0], base[1])
    b_im = (base[2], base[3])
    sign_b = jnp.where(lax.broadcasted_iota(jnp.int32, (8, bins), 0) < 4, 1.0, -1.0).astype(F32)
    sign_k = jnp.where(lax.broadcasted_iota(jnp.int32, (8, nb), 0) < 4, 1.0, -1.0).astype(F32)
    for sweep in range(2):
        a, b = short_product(chunk, (b_re, b_im), NT)
        kout[sweep] = a + sign_k * pltpu.roll(b, 4, 0)
        copies = [
            push(kout.at[sweep], kin.at[sweep, i], k_s.at[sweep, i], k_r.at[sweep, i], (x, y, p, q))
            for i, (p, q) in enumerate(fs)
        ]
        arrived(copies)
        proj = kout[sweep]
        for i in range(len(fs)):
            proj = proj + kin[sweep, i]
        a, b = short_product(proj, (b_re, b_im), NN)
        chunk = chunk - (a - sign_b * pltpu.roll(b, 4, 0))

    mine = x * ny + y
    pall[chunk_of(mine, 8), :] = chunk
    copies = [
        push(pall.at[chunk_of(mine, 8)], pall.at[chunk_of(mine, 8)], ay_s.at[i], ay_r.at[i], (x, p, z, c))
        for i, p in enumerate(ys)
    ]
    arrived(copies)
    copies = [
        push(pall.at[chunk_of(x, span)], pall.at[chunk_of(x, span)], ax_s.at[i], ax_r.at[i], (p, y, z, c))
        for i, p in enumerate(xs)
    ]
    live_halves = halves(live[...])
    arrived(copies)

    sign = jnp.where(is_im == 0, 1.0, -1.0).astype(F32)
    for half, both in enumerate((halves(sign * pall[...]), halves(swapped(pall[...], is_im, 0)))):
        for i in range(2):
            wt[i, :, half * bins : (half + 1) * bins] = both[i]

    npiv = emb // 2
    to_row = lax.broadcasted_iota(jnp.int32, (npiv, emb), 0)
    from_row = lax.broadcasted_iota(jnp.int32, (npiv, emb), 1)
    real_row = (to_row // 4) * 8 + lax.rem(to_row, 4)
    take_real = (from_row == real_row).astype(F32).astype(BF16)
    take_imag = (from_row == real_row + 4).astype(F32).astype(BF16)
    w = (wt[0], wt[1])
    top = tuple(dot(take_real, half, NN).astype(BF16) for half in w)
    gram = product(top, w, NT)
    gr = npiv // (nz * nc)
    cr = rows // (nz * nc)
    for i in range(nc):
        for j in range(nz):
            at = (i * nz + j) * gr
            gpart[i, j] = gram[at : at + gr]
    g_pair = push(gpart.at[1 - c], gpair, p_s.at[0], p_r.at[0], (x, y, z, 1 - c))
    cross = product(live_halves, w, NT)
    for i in range(nc):
        for j in range(nz):
            at = (i * nz + j) * cr
            cpart[i, j] = cross[at : at + cr]
    c_pair = push(cpart.at[1 - c], cpair, p_s.at[1], p_r.at[1], (x, y, z, 1 - c))

    def scatter(pair, part, got, half, inward, s, r):
        arrived([pair])
        half[...] = part[c] + got[...]
        return [push(half.at[p], inward.at[i], s.at[i], r.at[i], (x, y, p, c)) for i, p in enumerate(zs)]

    def spread(copies, half, inward, full, s, r):
        arrived(copies)
        total = half[z]
        for i in range(nz - 1):
            total = total + inward[i]
        full[c, z] = total
        return [push(full.at[c, z], full.at[c, z], s.at[i], r.at[i], (x, y, p, c)) for i, p in enumerate(zs)]

    g_scatter = scatter(g_pair, gpart, gpair, ghalf, gin, gz_s, gz_r)
    c_scatter = scatter(c_pair, cpart, cpair, chalf, cin, cz_s, cz_r)
    g_spread = spread(g_scatter, ghalf, gin, gfull, gt_s, gt_r)
    c_spread = spread(c_scatter, chalf, cin, cfull, ct_s, ct_r)
    arrived(g_spread)
    g_last = push(gfull.at[c], gfull.at[c], gc_s.at[0], gc_r.at[0], (x, y, z, 1 - c))
    arrived(c_spread)
    c_last = push(cfull.at[c], cfull.at[c], cc_s.at[0], cc_r.at[0], (x, y, z, 1 - c))
    arrived([g_last])

    gram = gfull[...].reshape(npiv, emb)
    col_part = lax.rem(lax.broadcasted_iota(jnp.int32, (npiv, emb), 1), 8) // 4
    turned = jnp.where(col_part == 0, -1.0, 1.0).astype(F32) * swapped(gram, col_part, 1)
    place = jnp.concatenate([take_real, take_imag], axis=0)
    spread_rows = jnp.concatenate([gram, turned], axis=0)
    parts = thirds(spread_rows)
    gram = sum(dot(place, part, ((0,), (0,))) for part in parts)
    eye = lax.broadcasted_iota(jnp.int32, (emb, emb), 0) == lax.broadcasted_iota(jnp.int32, (emb, emb), 1)
    ident = eye.astype(F32)
    diag = gram * ident
    scale_col = 1.0 / jnp.sqrt(jnp.sum(diag, axis=1, keepdims=True) + EPSILON)
    scale_row = 1.0 / jnp.sqrt(jnp.sum(diag, axis=0, keepdims=True) + EPSILON)
    gram = gram * (scale_col * scale_row)
    bound = jnp.max(jnp.sum(jnp.abs(gram), axis=1, keepdims=True), axis=0, keepdims=True)
    your = gram / bound
    zed = None
    for step in range(NS_STEPS):
        yh = halves(your)
        mix = your if zed is None else product(halves(zed), yh, NN)
        s = 1.5 * ident - 0.5 * mix
        sh = halves(s)
        if step < NS_STEPS - 1:
            your = product(yh, sh, NN)
        zed = s if zed is None else product(sh, halves(zed), NN)
    zed = zed * (1.0 / jnp.sqrt(bound))

    zed_out = tuple(dot(place, half, NN).astype(BF16) for half in halves(zed))
    arrived([c_last])
    cross = cfull[...].reshape(rows, emb)
    coef = product(halves(cross * scale_row), zed_out, NT)
    coef_re[...] = coef[:, :npiv]
    coef_im[...] = coef[:, npiv:]
    block = product(halves((zed_out[0].astype(F32) + zed_out[1].astype(F32)) * scale_row), w, NN)
    block = halves(block)
    ones = jnp.ones((8, 2 * bins), BF16)
    for r in range(0, rows, 64):
        part = slice(r, min(r + 64, rows))
        count = part.stop - part.start
        at = first_bin + lax.broadcasted_iota(jnp.int32, (count, bins), 1)
        mask = (at < BIN_BLOCK * lens[part, :]).astype(F32)
        back = product(halves(coef[part, :]), block, NN)
        new_re[part, :] = (live[part, :bins] - back[:, :bins]) * mask
        new_im[part, :] = (live[part, bins:] - back[:, bins:]) * mask
    squares = [thirds(ref[...] * ref[...]) for ref in (new_re, new_im)]
    summed = sum(dot(ones[:, :bins], p, NT) for three in squares for p in three)
    eout[...] = summed[0:1, :]
    here = f
    ein[here] = eout[...]
    copies = [
        push(eout, ein.at[here], e_s.at[i], e_r.at[i], (x, y, p, q)) for i, (p, q) in enumerate(fs)
    ]
    arrived(copies)
    total = ein[0]
    for i in range(1, nz * nc):
        total = total + ein[i]
    err[...] = total / (BIN_BLOCK * lens_row[...]).astype(F32)

    for copy in started:
        copy.wait_send()


def body(torus, res_re, res_im, basis_re, basis_im, lengths, pivots):
    nx, ny, nz, nc = torus
    rows, bins = res_re.shape
    nb = basis_re.shape[0]
    owners = nx * ny
    emb = 8 * owners
    nf = nz * nc
    piv = jnp.broadcast_to(pivots.reshape(owners, 1, 4), (owners, 2, 4)).reshape(emb, 1)
    gr = emb // 2 // nf
    cr = rows // nf
    vmem = pltpu.VMEM
    dma = pltpu.SemaphoreType.DMA
    out = [
        jax.ShapeDtypeStruct((rows, emb // 2), F32),
        jax.ShapeDtypeStruct((rows, emb // 2), F32),
        jax.ShapeDtypeStruct((rows, bins), F32),
        jax.ShapeDtypeStruct((rows, bins), F32),
        jax.ShapeDtypeStruct((1, rows), F32),
    ]
    scratch = [
        vmem((rows, 2 * bins), F32),
        vmem((4, nb, bins), BF16),
        vmem((emb, bins), F32),
        vmem((nx - 1, 8 * ny, bins), F32),
        vmem((8 * ny, bins), F32),
        vmem((ny - 1, 8, bins), F32),
        vmem((2, 8, nb), F32),
        vmem((2, nf - 1, 8, nb), F32),
        vmem((emb, bins), F32),
        vmem((2, emb, 2 * bins), BF16),
        vmem((nc, nz, gr, emb), F32), vmem((nz, gr, emb), F32), vmem((nz, gr, emb), F32),
        vmem((nz - 1, gr, emb), F32), vmem((nc, nz, gr, emb), F32),
        vmem((nc, nz, cr, emb), F32), vmem((nz, cr, emb), F32), vmem((nz, cr, emb), F32),
        vmem((nz - 1, cr, emb), F32), vmem((nc, nz, cr, emb), F32),
        vmem((1, rows), F32), vmem((nf, 1, rows), F32),
        dma((nx - 1,)), dma((nx - 1,)), dma((ny - 1,)), dma((ny - 1,)),
        dma((2, nf - 1)), dma((2, nf - 1)),
        dma((ny - 1,)), dma((ny - 1,)), dma((nx - 1,)), dma((nx - 1,)),
        dma((2,)), dma((2,)),
        dma((nz - 1,)), dma((nz - 1,)), dma((nz - 1,)), dma((nz - 1,)), dma((1,)), dma((1,)),
        dma((nz - 1,)), dma((nz - 1,)), dma((nz - 1,)), dma((nz - 1,)), dma((1,)), dma((1,)),
        dma((nf - 1,)), dma((nf - 1,)),
    ]
    whole = pl.BlockSpec(memory_space=pltpu.VMEM)
    coef_re, coef_im, new_re, new_im, err = pl.pallas_call(
        functools.partial(kernel, torus),
        out_shape=out,
        in_specs=[whole] * 7,
        out_specs=[whole] * 5,
        scratch_shapes=scratch,
        compiler_params=pltpu.CompilerParams(collective_id=0, has_side_effects=True),
    )(res_re, res_im, basis_re, basis_im, lengths[:, None], lengths[None, :], piv)
    return coef_re, coef_im, new_re, new_im, err.reshape(rows)


def build(mesh, torus):
    axes = Mesh(mesh.devices.reshape(torus), AXES)
    wave, freq = ("x", "y"), ("z", "core")
    in_specs = (P(wave, freq), P(wave, freq), P(None, freq), P(None, freq), P(wave), P())
    out_specs = (P(wave, None), P(wave, None), P(wave, freq), P(wave, freq), P(wave))
    return jax.shard_map(
        functools.partial(body, torus), mesh=axes, in_specs=in_specs, out_specs=out_specs, check_vma=False
    )


def solution(mesh):
    return build(mesh, TORUS)
```

time: 230 us -> 96.9 us (0.42)
  blocking collectives: 147 us -> 0 us
  Pallas kernels: 0 us -> 87.9 us
  matrix products: 35.5 us -> 0 us
  waiting for transfers between devices: 20.2 us -> 0 us
  starting transfers between devices: 14 us -> 0 us
  other arithmetic: 3.62 us -> 0 us
    all_to_all x8 -> x0, blocking collectives: 110 us -> none  [the longest x3 45.2 us: sum_at_owner(): lax.all_to_all(cut_along(shard, dim, peers), axis, 0, 0, tiled=True)]
    pallas_call x0 -> x1, Pallas kernels: none -> 87.9 us  [body(): pl.pallas_call(functools.partial(kernel, torus), out_shape=out, in_specs=...]
    all_gather x1 -> x0, blocking collectives: 37 us -> none  [sent_together(): lax.all_gather(both, axis, axis=dim, tiled=True)]
    dot_general x100 -> x0, matrix products: 35.5 us -> none  [the longest x84 27 us: plain(): jnp.dot(left, right, precision=lax.Precision.HIGHEST, preferred_element_t...]
    all_to_all x2 -> x0, waiting for transfers between devices: 20.2 us -> none  [the longest x1 11.7 us: sum_at_owner(): lax.all_to_all(cut_along(shard, dim, peers), axis, 0, 0, tiled=True)]
    all_to_all x2 -> x0, starting transfers between devices: 14 us -> none  [the longest x1 10.6 us: sum_at_owner(): lax.all_to_all(cut_along(shard, dim, peers), axis, 0, 0, tiled=True)]
    unnamed x24 -> x15, local copies, waits for them, and re-layouts: 1.59 us -> 6.44 us
  transfers between devices with their start and end apart: 2 -> 0, of which waited for: 2 -> 0; matrix products, arithmetic and copies ran while one was open for 1% -> 0% of each run, Pallas kernels for 0% -> 0%
where the time goes in v1:
time: 96.9 us; the launch traced here: 96.7 us
  Pallas kernels  87.9 us (91%)
  local copies, waits for them, and re-layouts  8.12 us (8%)
    pallas_call x1, Pallas kernels, body(): pl.pallas_call(functools.partial(kernel, torus), out_shape=out, in_specs=...  87.9 us
    unnamed x15, local copies, waits for them, and re-layouts  6.44 us

profile of v1, /device:TPU:1, one launch (start us, length us, event | category | flops | bytes accessed | tf_op | source)
XLA Modules:
  0.0 96.7 jit_solution(12201011579103421428)
XLA Ops:
  0.6 0.0 copy-start.4
  0.6 0.6 copy-done.4
  1.3 0.1 broadcast_in_dim.15
  1.4 0.0 copy-start.2
  1.4 0.8 reshape.20.piv
  2.2 0.0 copy-done.2
  2.2 0.8 copy.11.lens
  3.0 87.9 %shard_map.101 = (f32[256,128]{1,0:T(8,128)}, f32[256,128]{1,0:T(8,128)}, f32[256,512]{1,0:T(8,128)}, f32[256,512]{1,0:T(8,128)}, f32[1,256]{1,0:T(1,128)}) custom-call(f32[256,512]{1,0:T(8,128)} %res_re.1, f32[256,512]{1,0:T(8,128)} %res_im.1, f32[256,512]{1,0:T(8,128)} %basis_re.1, f32[256,512]{1,0:T(8,128)} %basis_im.1, s32[256,1]{1,0:T(8,128)} %copy.11.lens, ...), custom_call_target="tpu_custom_call" | custom-call | tf_op jit(solution)/shard_map/pallas_call | solution.py:336
  90.9 0.0 copy-start.1
  90.9 1.6 %copy.18 = f32[256,128]{1,0:T(8,128)} copy(f32[256,128]{1,0:T(8,128)} %get-tuple-element.20) | data formatting | bytes 262144
  92.5 1.6 %copy.19 = f32[256,128]{1,0:T(8,128)} copy(f32[256,128]{1,0:T(8,128)} %get-tuple-element.21) | data formatting | bytes 262144
  94.1 0.0 copy-done.1
  94.1 0.0 copy-start
  94.1 0.8 copy.20
  94.9 0.4 copy-done
  95.3 0.0 copy-start.3
  95.3 0.8 copy.21
  96.1 0.0 copy-done.3
  96.1 0.6 copy.22
  (1 shorter events, 0.0 us)
Async XLA Ops:
  0.6 0.7 copy-start.4
  1.4 0.8 copy-start.2
  90.9 3.2 %copy-start.1 = (f32[256,512]{1,0:T(8,128)S(1)}, f32[256,512]{1,0:T(8,128)}, u32[]{:S(2)}) copy-start(f32[256,512]{1,0:T(8,128)} %get-tuple-element.22) | copy-start | bytes 1572868
  94.1 1.2 %copy-start = (f32[256,512]{1,0:T(8,128)S(1)}, f32[256,512]{1,0:T(8,128)}, u32[]{:S(2)}) copy-start(f32[256,512]{1,0:T(8,128)} %get-tuple-element.23) | copy-start | bytes 1572868
  95.3 0.8 copy-start.3

commit v2 on v1

v2 whole, which is shorter than its diff:
```python
import functools

import jax
import jax.numpy as jnp
from jax import lax
from jax.experimental import pallas as pl
from jax.experimental.pallas import tpu as pltpu
from jax.sharding import Mesh
from jax.sharding import PartitionSpec as P

BIN_BLOCK = 128
NS_STEPS = 6
EPSILON = 1e-06
TORUS = (4, 8, 8, 2)
AXES = ("x", "y", "z", "core")
F32 = jnp.float32
BF16 = jnp.bfloat16


def dot(left, right, dims):
    return lax.dot_general(left, right, (dims, ((), ())), preferred_element_type=F32)


NN = ((1,), (0,))
NT = ((1,), (1,))


def halves(a):
    high = a.astype(BF16)
    return high, (a - high.astype(F32)).astype(BF16)


def thirds(a):
    high = a.astype(BF16)
    rest = a - high.astype(F32)
    mid = rest.astype(BF16)
    return high, mid, (rest - mid.astype(F32)).astype(BF16)


def product(left, right, dims):
    lh, ll = left
    rh, rl = right
    along = dims[1][0]
    return dot(jnp.concatenate([lh, ll, lh], axis=1), jnp.concatenate([rh, rh, rl], axis=along), dims)


def chosen(select, a):
    parts = thirds(a)
    return dot(jnp.concatenate([select] * 3, axis=1), jnp.concatenate(parts, axis=0), NN)


def swapped(a, part, axis):
    n = a.shape[axis]
    return jnp.where(part == 0, pltpu.roll(a, n - 4, axis), pltpu.roll(a, 4, axis))


def short_product(chunk, rights, dims):
    high = chunk.astype(BF16).astype(F32)
    both = jnp.concatenate([high, chunk - high], axis=0).astype(BF16)
    out = []
    for rh, rl in rights:
        a = dot(both, rh, dims)
        b = dot(both, rl, dims)
        out.append((a[:8] + a[8:]) + (b[:8] + b[8:]))
    return out


def kernel(
    torus,
    res_re, res_im, basis_re, basis_im, lens, piv,
    coef_re, coef_im, new_re, new_im, err,
    live, live_h, basis, base, vlen, vpiv, picked, far, relay, near, ysum, yr, kout, kin, pall, tall, wt,
    xpart, xpair, xhalf, xin, xfull,
    gpart, gpair, ghalf, gin, gfull, cpart, cpair, chalf, cin, cfull, eout, ein,
    in_s, rx_s, rx_r, ry_s, ry_r, k_s, k_r, p_s, p_r, py_s, py_r, px_s, px_r, pr_s, pr_r,
    ty_s, ty_r, tx_s, tx_r, tr_s, tr_r, zs_s, zs_r, zg_s, zg_r, c_s, c_r, e_s, e_r,
):
    nx, ny, nz, nc = torus
    x, y, z, c = (lax.axis_index(a) for a in AXES)
    f = z * nc + c
    rows, bins = res_re.shape
    emb = 8 * nx * ny
    npiv = emb // 2
    nb = basis_re.shape[0]
    span = 8 * ny
    right, left = lax.rem(x + 1, nx), lax.rem(x + nx - 1, nx)
    across = lax.rem(x + 2, nx)
    ys = [lax.rem(y + d, ny) for d in range(1, ny)]
    zs = [lax.rem(z + d, nz) for d in range(1, nz)]
    fs = [(lax.rem(z + dz, nz), lax.rem(c + dc, nc)) for dz in range(nz) for dc in range(nc) if dz or dc]

    loads = [(lens, vlen), (piv, vpiv), (res_re, live.at[:, pl.ds(0, bins)]), (res_im, live.at[:, pl.ds(bins, bins)])]
    loads += [(basis_re, basis.at[0]), (basis_im, basis.at[1])]
    loads = [pltpu.make_async_copy(src, dst, in_s.at[i]) for i, (src, dst) in enumerate(loads)]
    for load in loads:
        load.start()
    barrier = pltpu.get_barrier_semaphore()
    peers = [(right, y, z, c), (left, y, z, c)] + [(x, p, z, c) for p in ys] + [(x, y, p, q) for p, q in fs]
    for peer in peers:
        pl.semaphore_signal(barrier, inc=1, device_id=peer, device_id_type=pl.DeviceIdType.MESH)

    started = []

    def push(src, dst, send, recv, to):
        copy = pltpu.make_async_remote_copy(
            src_ref=src, dst_ref=dst, send_sem=send, recv_sem=recv, device_id=to,
            device_id_type=pl.DeviceIdType.MESH,
        )
        copy.start()
        started.append(copy)
        return copy

    def arrived(copies):
        for copy in copies:
            copy.wait_recv()

    def chunk_of(i, size):
        return pl.ds(pl.multiple_of(i * size, size), size)

    for load in loads[:4]:
        load.wait()
    diagonal = lax.broadcasted_iota(jnp.int32, (rows, rows), 0) == lax.broadcasted_iota(jnp.int32, (rows, rows), 1)
    ends = jnp.sum(jnp.where(diagonal, vlen[...] * BIN_BLOCK, 0).astype(F32), axis=1, keepdims=True)
    first_bin = f * bins

    def mask_of(part):
        count = part.stop - part.start
        at = first_bin + lax.broadcasted_iota(jnp.int32, (count, bins), 1)
        return (at.astype(F32) < ends[part, :]).astype(F32)

    blocks = [slice(r, min(r + 64, rows)) for r in range(0, rows, 64)]
    for part in blocks:
        mask = mask_of(part)
        live[part, :bins] = live[part, :bins] * mask
        live[part, bins:] = live[part, bins:] * mask
    to_row = lax.broadcasted_iota(jnp.int32, (emb, npiv), 0)
    of_row = lax.broadcasted_iota(jnp.int32, (emb, npiv), 1) == (to_row // 8) * 4 + lax.rem(to_row, 4)
    wanted = jnp.sum(jnp.where(of_row, vpiv[...], 0).astype(F32), axis=1, keepdims=True)
    own = (x * ny + y) * rows + lax.broadcasted_iota(jnp.int32, (emb, rows), 1)
    select = (wanted == own.astype(F32)).astype(F32).astype(BF16)
    is_im = lax.rem(lax.broadcasted_iota(jnp.int32, (emb, bins), 0), 8) // 4
    picked[...] = jnp.where(is_im == 0, chosen(select, live[:, :bins]), chosen(select, live[:, bins:]))

    pl.semaphore_wait(barrier, len(peers))

    half = bins // 2
    ahead, behind = pl.ds(0, half), pl.ds(half, half)
    to_right, to_left = (right, y, z, c), (left, y, z, c)
    far_copies = [
        push(picked.at[chunk_of(across, span), ahead], far.at[0], rx_s.at[0], rx_r.at[0], to_right),
        push(picked.at[chunk_of(across, span), behind], far.at[1], rx_s.at[1], rx_r.at[1], to_left),
    ]
    near_copies = [
        push(picked.at[chunk_of(right, span), behind], near.at[0, :, behind], rx_s.at[2], rx_r.at[2], to_right),
        push(picked.at[chunk_of(left, span), ahead], near.at[1, :, ahead], rx_s.at[3], rx_r.at[3], to_left),
    ]

    for load in loads[4:]:
        load.wait()
    for i in range(2):
        high, low = halves(basis[i])
        base[2 * i] = high
        base[2 * i + 1] = low
    b_re = (base[0], base[1])
    b_im = (base[2], base[3])
    plus = jnp.concatenate([basis[0] + basis[1], basis[1] - basis[0]], axis=1)
    right_side = tuple(jnp.concatenate([base[i], base[2 + i]], axis=1) for i in range(2))
    both = product(halves(plus), right_side, NT)

    def scatter_rows(part, value):
        size = part.shape[2]
        for i in range(nc):
            for j in range(nz):
                at = (i * nz + j) * size
                part[i, j] = value[at : at + size]

    def pair_up(k, part, got):
        return push(part.at[1 - c], got, p_s.at[k], p_r.at[k], (x, y, z, 1 - c))

    def scatter(k, pair, part, got, summed, inward):
        arrived([pair])
        summed[...] = part[c] + got[...]
        return [push(summed.at[p], inward.at[i], zs_s.at[k, i], zs_r.at[k, i], (x, y, p, c)) for i, p in enumerate(zs)]

    def spread(k, copies, summed, inward, full):
        arrived(copies)
        total = summed[z]
        for i in range(nz - 1):
            total = total + inward[i]
        full[c, z] = total
        return [push(full.at[c, z], full.at[c, z], zg_s.at[k, i], zg_r.at[k, i], (x, y, p, c)) for i, p in enumerate(zs)]

    def share(k, copies, full):
        arrived(copies)
        return push(full.at[c], full.at[c], c_s.at[k], c_r.at[k], (x, y, z, 1 - c))

    scatter_rows(xpart, both)
    x_pair = pair_up(0, xpart, xpair)

    arrived(far_copies[:1])
    relay[0] = picked[chunk_of(right, span), :half] + far[0]
    near_copies.append(push(relay.at[0], near.at[0, :, ahead], rx_s.at[4], rx_r.at[4], to_right))
    arrived(far_copies[1:])
    relay[1] = picked[chunk_of(left, span), half:] + far[1]
    near_copies.append(push(relay.at[1], near.at[1, :, behind], rx_s.at[5], rx_r.at[5], to_left))
    x_scatter = scatter(0, x_pair, xpart, xpair, xhalf, xin)
    arrived(near_copies)
    ysum[...] = picked[chunk_of(x, span), :] + near[0] + near[1]
    y_copies = [
        push(ysum.at[chunk_of(p, 8)], yr.at[i], ry_s.at[i], ry_r.at[i], (x, p, z, c)) for i, p in enumerate(ys)
    ]
    for i, value in enumerate(halves(live[...])):
        live_h[i] = value
    x_spread = spread(0, x_scatter, xhalf, xin, xfull)
    arrived(y_copies)
    chunk = ysum[chunk_of(y, 8), :]
    for i in range(ny - 1):
        chunk = chunk + yr[i]

    mine = x * ny + y
    order = sorted(range(1, ny), key=lambda d: min(d, ny - d))

    def gather_steps(buf, ss, rs, wide):
        ysend, xsend, rsend = ss
        yrecv, xrecv, rrecv = rs
        lanes = (pl.ds(0, wide // 2), pl.ds(wide // 2, wide // 2))
        copies = {}

        def rows_of(i, d):
            return pl.ds(pl.multiple_of((i * ny + lax.rem(y + ny - d, ny)) * 8, 8), 8)

        def along_y():
            at = chunk_of(mine, 8)
            for i, p in enumerate(ys):
                copies["y", i + 1] = push(buf.at[at], buf.at[at], ysend.at[i], yrecv.at[i], (x, p, z, c))

        def along_x(d):
            if d:
                arrived([copies["y", d]])
            at = rows_of(x, d)
            for k, to in enumerate((to_right, to_left)):
                copies["x", d, k] = push(buf.at[at], buf.at[at], xsend.at[d, k], xrecv.at[d, k], to)

        def further(d):
            for k, (source, to) in enumerate(((left, to_right), (right, to_left))):
                arrived([copies["x", d, k]])
                at = rows_of(source, d)
                copies["r", d, k] = push(
                    buf.at[at, lanes[k]], buf.at[at, lanes[k]], rsend.at[d, k], rrecv.at[d, k], to
                )

        def finish():
            arrived([copies["r", d, k] for d in range(ny) for k in range(2)])

        return along_y, along_x, further, finish

    pall[chunk_of(mine, 8), :] = chunk
    p_y, p_x, p_further, p_finish = gather_steps(pall, (py_s, px_s, pr_s), (py_r, px_r, pr_r), bins)
    p_y()
    p_x(0)
    sign_k = jnp.where(lax.broadcasted_iota(jnp.int32, (8, nb), 0) < 4, 1.0, -1.0).astype(F32)
    a, b = short_product(chunk, (b_re, b_im), NT)
    kout[...] = a + sign_k * pltpu.roll(b, 4, 0)
    k_copies = [
        push(kout, kin.at[i], k_s.at[i], k_r.at[i], (x, y, p, q)) for i, (p, q) in enumerate(fs)
    ]
    x_last = share(0, x_spread, xfull)
    for d in order:
        p_x(d)
    late = [0] + order
    early, late = late[:3], late[3:]
    for d in early:
        p_further(d)
    arrived([x_last])
    arrived(k_copies)
    proj = kout[...]
    for i in range(len(fs)):
        proj = proj + kin[i]
    gram = halves(xfull[...].reshape(nb, nb))
    (straight,) = short_product(proj, (gram,), NN)
    (turned,) = short_product(proj, (gram,), NT)
    again = 0.5 * ((straight + turned) - sign_k * pltpu.roll(straight - turned, 4, 0))
    tall[chunk_of(mine, 8), :] = 2.0 * proj - again
    t_y, t_x, t_further, t_finish = gather_steps(tall, (ty_s, tx_s, tr_s), (ty_r, tx_r, tr_r), nb)
    t_y()
    t_x(0)
    for d in late:
        p_further(d)
    for d in order[:2]:
        t_x(d)
    t_further(0)
    for d in order[2:]:
        t_x(d)
    for d in order:
        t_further(d)
    p_finish()
    t_finish()

    sign = jnp.where(is_im == 0, 1.0, -1.0).astype(F32)
    taken = halves(tall[...])
    back = product(taken, b_re, NN) - sign * swapped(product(taken, b_im, NN), is_im, 0)
    ortho = pall[...] - back
    for k, two in enumerate((halves(sign * ortho), halves(swapped(ortho, is_im, 0)))):
        for i in range(2):
            wt[i, :, k * bins : (k + 1) * bins] = two[i]

    to_row = lax.broadcasted_iota(jnp.int32, (npiv, emb), 0)
    from_row = lax.broadcasted_iota(jnp.int32, (npiv, emb), 1)
    real_row = (to_row // 4) * 8 + lax.rem(to_row, 4)
    take_real = (from_row == real_row).astype(F32).astype(BF16)
    take_imag = (from_row == real_row + 4).astype(F32).astype(BF16)
    w = (wt[0], wt[1])
    top = tuple(dot(take_real, part, NN).astype(BF16) for part in w)
    scatter_rows(gpart, product(top, w, NT))
    g_pair = pair_up(1, gpart, gpair)
    scatter_rows(cpart, product((live_h[0], live_h[1]), w, NT))
    c_pair = pair_up(2, cpart, cpair)

    g_scatter = scatter(1, g_pair, gpart, gpair, ghalf, gin)
    c_scatter = scatter(2, c_pair, cpart, cpair, chalf, cin)
    g_spread = spread(1, g_scatter, ghalf, gin, gfull)
    c_spread = spread(2, c_scatter, chalf, cin, cfull)
    g_last = share(1, g_spread, gfull)
    arrived([g_last])

    gram = gfull[...].reshape(npiv, emb)
    col_part = lax.rem(lax.broadcasted_iota(jnp.int32, (npiv, emb), 1), 8) // 4
    turned = jnp.where(col_part == 0, -1.0, 1.0).astype(F32) * swapped(gram, col_part, 1)
    place = jnp.concatenate([take_real, take_imag], axis=0)
    parts = thirds(jnp.concatenate([gram, turned], axis=0))
    gram = sum(dot(place, part, ((0,), (0,))) for part in parts)
    eye = lax.broadcasted_iota(jnp.int32, (emb, emb), 0) == lax.broadcasted_iota(jnp.int32, (emb, emb), 1)
    ident = eye.astype(F32)
    diag = gram * ident
    scale_col = 1.0 / jnp.sqrt(jnp.sum(diag, axis=1, keepdims=True) + EPSILON)
    scale_row = 1.0 / jnp.sqrt(jnp.sum(diag, axis=0, keepdims=True) + EPSILON)
    gram = gram * (scale_col * scale_row)
    bound = jnp.max(jnp.sum(jnp.abs(gram), axis=1, keepdims=True), axis=0, keepdims=True)
    your = gram / bound
    zed = None
    for step in range(NS_STEPS):
        if step == 3:
            c_last = share(2, c_spread, cfull)
        yh = halves(your)
        mix = your if zed is None else product(halves(zed), yh, NN)
        s = 1.5 * ident - 0.5 * mix
        sh = halves(s)
        if step < NS_STEPS - 1:
            your = product(yh, sh, NN)
        zed = s if zed is None else product(sh, halves(zed), NN)
    zed = zed * (1.0 / jnp.sqrt(bound))

    zed_out = tuple(dot(place, part, NN).astype(BF16) for part in halves(zed))
    block = product(halves((zed_out[0].astype(F32) + zed_out[1].astype(F32)) * scale_row), w, NN)
    block = halves(block)
    arrived([c_last])
    cross = cfull[...].reshape(rows, emb)
    coef = product(halves(cross * scale_row), zed_out, NT)
    coef_re[...] = coef[:, :npiv]
    coef_im[...] = coef[:, npiv:]
    sums = []
    for part in blocks:
        mask = mask_of(part)
        back = product(halves(coef[part, :]), block, NN)
        real = (live[part, :bins] - back[:, :bins]) * mask
        imag = (live[part, bins:] - back[:, bins:]) * mask
        new_re[part, :] = real
        new_im[part, :] = imag
        square = real * real + imag * imag
        sums.append(sum(square[:, i : i + 128] for i in range(0, bins, 128)))
    ones = jnp.ones((8, 128), BF16)
    summed = sum(dot(ones, part, NT) for part in thirds(jnp.concatenate(sums, axis=0)))
    eout[...] = summed[0:1, :]
    ein[f] = summed[0:1, :]
    copies = [push(eout, ein.at[f], e_s.at[i], e_r.at[i], (x, y, p, q)) for i, (p, q) in enumerate(fs)]
    arrived(copies)
    total = ein[0]
    for i in range(1, nz * nc):
        total = total + ein[i]
    err[...] = total / (BIN_BLOCK * vlen[...]).astype(F32)

    for copy in started:
        copy.wait_send()


def handed_out(*refs):
    count = len(refs) // 2
    copies = [pltpu.make_async_copy(refs[i], refs[count + i], refs[-1].at[i]) for i in range(count)]
    for copy in copies:
        copy.start()
    for copy in copies:
        copy.wait()


def body(torus, res_re, res_im, basis_re, basis_im, lengths, pivots):
    nx, ny, nz, nc = torus
    rows, bins = res_re.shape
    nb = basis_re.shape[0]
    emb = 8 * nx * ny
    nf = nz * nc
    span = 8 * ny
    vmem = pltpu.VMEM
    dma = pltpu.SemaphoreType.DMA
    shapes = [(rows, emb // 2), (rows, emb // 2), (rows, bins), (rows, bins), (1, rows)]

    def summed(count, width):
        part = count // nf
        whole, across = vmem((nc, nz, part, width), F32), vmem((nz, part, width), F32)
        return [whole, across, across, vmem((nz - 1, part, width), F32), whole]

    scratch = [
        vmem((rows, 2 * bins), F32),
        vmem((2, rows, 2 * bins), BF16),
        vmem((2, nb, bins), F32),
        vmem((4, nb, bins), BF16),
        vmem((1, rows), jnp.int32),
        vmem((1, emb // 2), jnp.int32),
        vmem((emb, bins), F32),
        vmem((2, span, bins // 2), F32),
        vmem((2, span, bins // 2), F32),
        vmem((2, span, bins), F32),
        vmem((span, bins), F32),
        vmem((ny - 1, 8, bins), F32),
        vmem((8, nb), F32),
        vmem((nf - 1, 8, nb), F32),
        vmem((emb, bins), F32),
        vmem((emb, nb), F32),
        vmem((2, emb, 2 * bins), BF16),
        *summed(nb, nb),
        *summed(emb // 2, emb),
        *summed(rows, emb),
        vmem((1, rows), F32), vmem((nf, 1, rows), F32),
        dma((6,)), dma((6,)), dma((6,)), dma((ny - 1,)), dma((ny - 1,)), dma((nf - 1,)), dma((nf - 1,)),
        dma((3,)), dma((3,)),
        *[dma((ny - 1,)), dma((ny - 1,)), dma((ny, 2)), dma((ny, 2)), dma((ny, 2)), dma((ny, 2))] * 2,
        dma((3, nz - 1)), dma((3, nz - 1)), dma((3, nz - 1)), dma((3, nz - 1)), dma((3,)), dma((3,)),
        dma((nf - 1,)), dma((nf - 1,)),
    ]
    here = pl.BlockSpec(memory_space=pltpu.VMEM)
    there = pl.BlockSpec(memory_space=pl.ANY)
    results = pl.pallas_call(
        functools.partial(kernel, torus),
        out_shape=[vmem(shape, F32) for shape in shapes],
        in_specs=[there] * 6,
        out_specs=[here] * 5,
        scratch_shapes=scratch,
        compiler_params=pltpu.CompilerParams(collective_id=0, has_side_effects=True),
    )(res_re, res_im, basis_re, basis_im, lengths.reshape(1, rows), pivots.reshape(1, emb // 2))
    coef_re, coef_im, new_re, new_im, err = pl.pallas_call(
        handed_out,
        out_shape=[jax.ShapeDtypeStruct(shape, F32) for shape in shapes],
        in_specs=[here] * 5,
        out_specs=[there] * 5,
        scratch_shapes=[dma((5,))],
    )(*[pltpu.with_memory_space_constraint(result, pltpu.VMEM) for result in results])
    return coef_re, coef_im, new_re, new_im, err.reshape(rows)


def build(mesh, torus):
    axes = Mesh(mesh.devices.reshape(torus), AXES)
    wave, freq = ("x", "y"), ("z", "core")
    in_specs = (P(wave, freq), P(wave, freq), P(None, freq), P(None, freq), P(wave), P())
    out_specs = (P(wave, None), P(wave, None), P(wave, freq), P(wave, freq), P(wave))
    return jax.shard_map(
        functools.partial(body, torus), mesh=axes, in_specs=in_specs, out_specs=out_specs, check_vma=False
    )


def solution(mesh):
    return build(mesh, TORUS)
```

time: 96.9 us -> 79.5 us (0.82)
  Pallas kernels: 87.9 us -> 78.7 us
  local copies, waits for them, and re-layouts: 8.12 us -> 0 us
    pallas_call x1 -> x2, Pallas kernels: 87.9 us -> 78.7 us  [the longest x1 77.6 us: body(): pl.pallas_call(functools.partial(kernel, torus), out_shape=[vmem(shape, F...]
    unnamed x15 -> x0, local copies, waits for them, and re-layouts: 6.44 us -> none
where the time goes in v2:
time: 79.5 us; the launch traced here: 79.4 us
  Pallas kernels  78.7 us (99%)
    pallas_call x1, Pallas kernels, body(): pl.pallas_call(functools.partial(kernel, torus), out_shape=[vmem(shape, F...  77.6 us

profile of v2, /device:TPU:1, one launch (start us, length us, event | category | flops | bytes accessed | tf_op | source)
XLA Modules:
  0.0 79.4 jit_solution(18111602271242422084)
XLA Ops:
  0.6 77.6 %shard_map.101 = (f32[256,128]{1,0:T(8,128)S(1)}, f32[256,128]{1,0:T(8,128)S(1)}, f32[256,512]{1,0:T(8,128)S(1)}, f32[256,512]{1,0:T(8,128)S(1)}, f32[1,256]{1,0:T(1,128)S(1)}) custom-call(f32[256,512]{1,0:T(8,128)} %res_re.1, f32[256,512]{1,0:T(8,128)} %res_im.1, f32[256,512]{1,0:T(8,128)} %basis_re.1, f32[256,512]{1,0:T(8,128)} %basis_im.1, ...), custom_call_target="tpu_custom_call" | custom-call | tf_op jit(solution)/shard_map/pallas_call | solution.py:441
  78.3 1.1 %shard_map.102 = (f32[256,128]{1,0:T(8,128)}, f32[256,128]{1,0:T(8,128)}, f32[256,512]{1,0:T(8,128)}, f32[256,512]{1,0:T(8,128)}, f32[1,256]{1,0:T(1,128)}) custom-call(f32[256,128]{1,0:T(8,128)S(1)} %get-tuple-element.15.refs_0_, f32[256,128]{1,0:T(8,128)S(1)} %get-tuple-element.16.refs_1_, f32[256,512]{1,0:T(8,128)S(1)} %get-tuple-element.17.refs_2_, ...), custom_call_target="tpu_custom_call" | custom-call | tf_op jit(solution)/shard_map/pallas_call | solution.py:449

commit v3 on v2

--- a/solution.py
+++ b/solution.py
@@ -68,12 +68,13 @@
 def kernel(
     torus,
     res_re, res_im, basis_re, basis_im, lens, piv,
+    out_coef_re, out_coef_im, out_new_re, out_new_im, out_err,
+    live, live_h, basis, base, vlen, vpiv, picked, far, relay, near, ysum, yr, kout, kin, pall, kall, wt,
     coef_re, coef_im, new_re, new_im, err,
-    live, live_h, basis, base, vlen, vpiv, picked, far, relay, near, ysum, yr, kout, kin, pall, tall, wt,
     xpart, xpair, xhalf, xin, xfull,
-    gpart, gpair, ghalf, gin, gfull, cpart, cpair, chalf, cin, cfull, eout, ein,
+    gpart, gpair, ghalf, gin, gfull, cpart, cpair, chalf, cin, cfull, dpart, dpair, dhalf, din, eout, ein,
     in_s, rx_s, rx_r, ry_s, ry_r, k_s, k_r, p_s, p_r, py_s, py_r, px_s, px_r, pr_s, pr_r,
-    ty_s, ty_r, tx_s, tx_r, tr_s, tr_r, zs_s, zs_r, zg_s, zg_r, c_s, c_r, e_s, e_r,
+    kg_s, kg_r, zs_s, zs_r, zg_s, zg_r, c_s, c_r, e_s, e_r, out_s,
 ):
     nx, ny, nz, nc = torus
     x, y, z, c = (lax.axis_index(a) for a in AXES)
@@ -85,9 +86,20 @@
     span = 8 * ny
     right, left = lax.rem(x + 1, nx), lax.rem(x + nx - 1, nx)
     across = lax.rem(x + 2, nx)
-    ys = [lax.rem(y + d, ny) for d in range(1, ny)]
-    zs = [lax.rem(z + d, nz) for d in range(1, nz)]
-    fs = [(lax.rem(z + dz, nz), lax.rem(c + dc, nc)) for dz in range(nz) for dc in range(nc) if dz or dc]
+
+
+    def hops(d, n):
+        return min(d, n - d)
+
+    ys = [(d - 1, lax.rem(y + d, ny)) for d in sorted(range(1, ny), key=lambda d: -hops(d, ny))]
+    zs = [(d - 1, lax.rem(z + d, nz)) for d in sorted(range(1, nz), key=lambda d: -hops(d, nz))]
+    fs = sorted(((dz, dc) for dz in range(nz) for dc in range(nc) if dz or dc), key=lambda d: -hops(d[0], nz))
+    fs = [(dz * nc + dc - 1, (x, y, lax.rem(z + dz, nz), lax.rem(c + dc, nc))) for dz, dc in fs]
+    plane = sorted(
+        ((dx, dy) for dx in range(nx) for dy in range(ny) if dx or dy),
+        key=lambda d: -hops(d[0], nx) - hops(d[1], ny),
+    )
+    plane = [(dx * ny + dy - 1, (lax.rem(x + dx, nx), lax.rem(y + dy, ny), z, c)) for dx, dy in plane]
 
     loads = [(lens, vlen), (piv, vpiv), (res_re, live.at[:, pl.ds(0, bins)]), (res_im, live.at[:, pl.ds(bins, bins)])]
     loads += [(basis_re, basis.at[0]), (basis_im, basis.at[1])]
@@ -95,7 +107,7 @@
     for load in loads:
         load.start()
     barrier = pltpu.get_barrier_semaphore()
-    peers = [(right, y, z, c), (left, y, z, c)] + [(x, p, z, c) for p in ys] + [(x, y, p, q) for p, q in fs]
+    peers = [to for _, to in fs + plane]
     for peer in peers:
         pl.semaphore_signal(barrier, inc=1, device_id=peer, device_id_type=pl.DeviceIdType.MESH)
 
@@ -155,6 +167,8 @@
         push(picked.at[chunk_of(left, span), ahead], near.at[1, :, ahead], rx_s.at[3], rx_r.at[3], to_left),
     ]
 
+    for i, value in enumerate(halves(live[...])):
+        live_h[i] = value
     for load in loads[4:]:
         load.wait()
     for i in range(2):
@@ -180,15 +194,18 @@
     def scatter(k, pair, part, got, summed, inward):
         arrived([pair])
         summed[...] = part[c] + got[...]
-        return [push(summed.at[p], inward.at[i], zs_s.at[k, i], zs_r.at[k, i], (x, y, p, c)) for i, p in enumerate(zs)]
-
-    def spread(k, copies, summed, inward, full):
+        return [push(summed.at[p], inward.at[i], zs_s.at[k, i], zs_r.at[k, i], (x, y, p, c)) for i, p in zs]
+
+    def gathered(copies, summed, inward):
         arrived(copies)
         total = summed[z]
         for i in range(nz - 1):
             total = total + inward[i]
+        return total
+
+    def spread(k, total, full):
         full[c, z] = total
-        return [push(full.at[c, z], full.at[c, z], zg_s.at[k, i], zg_r.at[k, i], (x, y, p, c)) for i, p in enumerate(zs)]
+        return [push(full.at[c, z], full.at[c, z], zg_s.at[k, i], zg_r.at[k, i], (x, y, p, c)) for i, p in zs]
 
     def share(k, copies, full):
         arrived(copies)
@@ -196,6 +213,11 @@
 
     scatter_rows(xpart, both)
     x_pair = pair_up(0, xpart, xpair)
+    turned_side = tuple(jnp.concatenate([-base[2 + i], base[i]], axis=1) for i in range(2))
+    both = tuple(jnp.concatenate([right_side[i], turned_side[i]], axis=0) for i in range(2))
+    scatter_rows(dpart, product((live_h[0], live_h[1]), both, NT))
+    x_scatter = scatter(0, x_pair, xpart, xpair, xhalf, xin)
+    d_pair = pair_up(3, dpart, dpair)
 
     arrived(far_copies[:1])
     relay[0] = picked[chunk_of(right, span), :half] + far[0]
@@ -203,15 +225,13 @@
     arrived(far_copies[1:])
     relay[1] = picked[chunk_of(left, span), half:] + far[1]
     near_copies.append(push(relay.at[1], near.at[1, :, behind], rx_s.at[5], rx_r.at[5], to_left))
-    x_scatter = scatter(0, x_pair, xpart, xpair, xhalf, xin)
+    d_scatter = scatter(3, d_pair, dpart, dpair, dhalf, din)
     arrived(near_copies)
     ysum[...] = picked[chunk_of(x, span), :] + near[0] + near[1]
     y_copies = [
-        push(ysum.at[chunk_of(p, 8)], yr.at[i], ry_s.at[i], ry_r.at[i], (x, p, z, c)) for i, p in enumerate(ys)
+        push(ysum.at[chunk_of(p, 8)], yr.at[i], ry_s.at[i], ry_r.at[i], (x, p, z, c)) for i, p in ys
     ]
-    for i, value in enumerate(halves(live[...])):
-        live_h[i] = value
-    x_spread = spread(0, x_scatter, xhalf, xin, xfull)
+    x_spread = spread(0, gathered(x_scatter, xhalf, xin), xfull)
     arrived(y_copies)
     chunk = ysum[chunk_of(y, 8), :]
     for i in range(ny - 1):
@@ -231,7 +251,7 @@
 
         def along_y():
             at = chunk_of(mine, 8)
-            for i, p in enumerate(ys):
+            for i, p in ys:
                 copies["y", i + 1] = push(buf.at[at], buf.at[at], ysend.at[i], yrecv.at[i], (x, p, z, c))
 
         def along_x(d):
@@ -261,9 +281,7 @@
     sign_k = jnp.where(lax.broadcasted_iota(jnp.int32, (8, nb), 0) < 4, 1.0, -1.0).astype(F32)
     a, b = short_product(chunk, (b_re, b_im), NT)
     kout[...] = a + sign_k * pltpu.roll(b, 4, 0)
-    k_copies = [
-        push(kout, kin.at[i], k_s.at[i], k_r.at[i], (x, y, p, q)) for i, (p, q) in enumerate(fs)
-    ]
+    k_copies = [push(kout, kin.at[i], k_s.at[i], k_r.at[i], to) for i, to in fs]
     x_last = share(0, x_spread, xfull)
     for d in order:
         p_x(d)
@@ -271,39 +289,28 @@
     early, late = late[:3], late[3:]
     for d in early:
         p_further(d)
-    arrived([x_last])
     arrived(k_copies)
     proj = kout[...]
     for i in range(len(fs)):
         proj = proj + kin[i]
-    gram = halves(xfull[...].reshape(nb, nb))
-    (straight,) = short_product(proj, (gram,), NN)
-    (turned,) = short_product(proj, (gram,), NT)
-    again = 0.5 * ((straight + turned) - sign_k * pltpu.roll(straight - turned, 4, 0))
-    tall[chunk_of(mine, 8), :] = 2.0 * proj - again
-    t_y, t_x, t_further, t_finish = gather_steps(tall, (ty_s, tx_s, tr_s), (ty_r, tx_r, tr_r), nb)
-    t_y()
-    t_x(0)
+    at = chunk_of(mine, 8)
+    kall[at, :] = proj
+    k_gather = [push(kall.at[at], kall.at[at], kg_s.at[i], kg_r.at[i], to) for i, to in plane]
     for d in late:
         p_further(d)
-    for d in order[:2]:
-        t_x(d)
-    t_further(0)
-    for d in order[2:]:
-        t_x(d)
-    for d in order:
-        t_further(d)
     p_finish()
-    t_finish()
 
     sign = jnp.where(is_im == 0, 1.0, -1.0).astype(F32)
-    taken = halves(tall[...])
-    back = product(taken, b_re, NN) - sign * swapped(product(taken, b_im, NN), is_im, 0)
-    ortho = pall[...] - back
-    for k, two in enumerate((halves(sign * ortho), halves(swapped(ortho, is_im, 0)))):
-        for i in range(2):
-            wt[i, :, k * bins : (k + 1) * bins] = two[i]
-
+    sign_all = jnp.where(
+        lax.rem(lax.broadcasted_iota(jnp.int32, (emb, nb), 0), 8) < 4, 1.0, -1.0
+    ).astype(F32)
+    part_all = lax.rem(lax.broadcasted_iota(jnp.int32, (emb, nb), 0), 8) // 4
+
+    def both_parts(a, signs, parts):
+        return halves(jnp.concatenate([signs * a, swapped(a, parts, 0)], axis=1))
+
+    for i, value in enumerate(both_parts(pall[...], sign, is_im)):
+        wt[i] = value
     to_row = lax.broadcasted_iota(jnp.int32, (npiv, emb), 0)
     from_row = lax.broadcasted_iota(jnp.int32, (npiv, emb), 1)
     real_row = (to_row // 4) * 8 + lax.rem(to_row, 4)
@@ -318,8 +325,30 @@
 
     g_scatter = scatter(1, g_pair, gpart, gpair, ghalf, gin)
     c_scatter = scatter(2, c_pair, cpart, cpair, chalf, cin)
-    g_spread = spread(1, g_scatter, ghalf, gin, gfull)
-    c_spread = spread(2, c_scatter, chalf, cin, cfull)
+    arrived([x_last])
+    arrived(k_gather)
+
+    inner = halves(xfull[...].reshape(nb, nb))
+
+    def times_inner(a):
+        both = halves(a)
+        straight, across = product(both, inner, NN), product(both, inner, NT)
+        return 0.5 * ((straight + across) - sign_all * swapped(straight - across, part_all, 0))
+
+    taken = 2.0 * kall[...] - times_inner(kall[...])
+    rest = both_parts(kall[...] - times_inner(taken), sign_all, part_all)
+    k_both = both_parts(kall[...], sign_all, part_all)
+    t_both = both_parts(taken, sign_all, part_all)
+    less = product(t_both, k_both, NT) + product(rest, t_both, NT)
+    g_spread = spread(1, gathered(g_scatter, ghalf, gin), gfull)
+    kept = gathered(d_scatter, dhalf, din)
+    total = gathered(c_scatter, chalf, cin)
+    c_spread = spread(2, total - product(halves(kept), t_both, NT), cfull)
+    taken = halves(taken)
+    back = product(taken, b_re, NN) - sign * swapped(product(taken, b_im, NN), is_im, 0)
+    for i, value in enumerate(both_parts(pall[...] - back, sign, is_im)):
+        wt[i] = value
+    w = (wt[0], wt[1])
     g_last = share(1, g_spread, gfull)
     arrived([g_last])
 
@@ -328,7 +357,7 @@
     turned = jnp.where(col_part == 0, -1.0, 1.0).astype(F32) * swapped(gram, col_part, 1)
     place = jnp.concatenate([take_real, take_imag], axis=0)
     parts = thirds(jnp.concatenate([gram, turned], axis=0))
-    gram = sum(dot(place, part, ((0,), (0,))) for part in parts)
+    gram = sum(dot(place, part, ((0,), (0,))) for part in parts) - less
     eye = lax.broadcasted_iota(jnp.int32, (emb, emb), 0) == lax.broadcasted_iota(jnp.int32, (emb, emb), 1)
     ident = eye.astype(F32)
     diag = gram * ident
@@ -372,15 +401,22 @@
     summed = sum(dot(ones, part, NT) for part in thirds(jnp.concatenate(sums, axis=0)))
     eout[...] = summed[0:1, :]
     ein[f] = summed[0:1, :]
-    copies = [push(eout, ein.at[f], e_s.at[i], e_r.at[i], (x, y, p, q)) for i, (p, q) in enumerate(fs)]
+    copies = [push(eout, ein.at[f], e_s.at[i], e_r.at[i], to) for i, to in fs]
+    results = [(coef_re, out_coef_re), (coef_im, out_coef_im), (new_re, out_new_re), (new_im, out_new_im), (err, out_err)]
+    results = [pltpu.make_async_copy(src, dst, out_s.at[i]) for i, (src, dst) in enumerate(results)]
+    for result in results[:4]:
+        result.start()
     arrived(copies)
     total = ein[0]
     for i in range(1, nz * nc):
         total = total + ein[i]
     err[...] = total / (BIN_BLOCK * vlen[...]).astype(F32)
+    results[4].start()
 
     for copy in started:
         copy.wait_send()
+    for result in results:
+        result.wait()
 
 
 def handed_out(*refs):
@@ -426,15 +462,18 @@
         vmem((emb, bins), F32),
         vmem((emb, nb), F32),
         vmem((2, emb, 2 * bins), BF16),
+        *[vmem(shape, F32) for shape in shapes],
         *summed(nb, nb),
         *summed(emb // 2, emb),
         *summed(rows, emb),
+        *summed(rows, 2 * nb)[:4],
         vmem((1, rows), F32), vmem((nf, 1, rows), F32),
         dma((6,)), dma((6,)), dma((6,)), dma((ny - 1,)), dma((ny - 1,)), dma((nf - 1,)), dma((nf - 1,)),
-        dma((3,)), dma((3,)),
-        *[dma((ny - 1,)), dma((ny - 1,)), dma((ny, 2)), dma((ny, 2)), dma((ny, 2)), dma((ny, 2))] * 2,
-        dma((3, nz - 1)), dma((3, nz - 1)), dma((3, nz - 1)), dma((3, nz - 1)), dma((3,)), dma((3,)),
-        dma((nf - 1,)), dma((nf - 1,)),
+        dma((4,)), dma((4,)),
+        dma((ny - 1,)), dma((ny - 1,)), dma((ny, 2)), dma((ny, 2)), dma((ny, 2)), dma((ny, 2)),
+        dma((nx * ny - 1,)), dma((nx * ny - 1,)),
+        dma((4, nz - 1)), dma((4, nz - 1)), dma((3, nz - 1)), dma((3, nz - 1)), dma((3,)), dma((3,)),
+        dma((nf - 1,)), dma((nf - 1,)), dma((5,)),
     ]
     here = pl.BlockSpec(memory_space=pltpu.VMEM)
     there = pl.BlockSpec(memory_space=pl.ANY)
@@ -442,7 +481,7 @@
         functools.partial(kernel, torus),
         out_shape=[vmem(shape, F32) for shape in shapes],
         in_specs=[there] * 6,
-        out_specs=[here] * 5,
+        out_specs=[there] * 5,
         scratch_shapes=scratch,
         compiler_params=pltpu.CompilerParams(collective_id=0, has_side_effects=True),
     )(res_re, res_im, basis_re, basis_im, lengths.reshape(1, rows), pivots.reshape(1, emb // 2))

time: 79.5 us -> 74.2 us (0.933)
  Pallas kernels: 78.7 us -> 73.4 us
    pallas_call x1, Pallas kernels: 77.6 us -> 72.3 us  [body(): pl.pallas_call(functools.partial(kernel, torus), out_shape=[vmem(shape, F...]
where the time goes in v3:
time: 74.2 us; the launch traced here: 74.1 us
  Pallas kernels  73.4 us (99%)
    pallas_call x1, Pallas kernels, body(): pl.pallas_call(functools.partial(kernel, torus), out_shape=[vmem(shape, F...  72.3 us

profile of v3, /device:TPU:1, one launch (start us, length us, event | category | flops | bytes accessed | tf_op | source)
XLA Modules:
  0.0 74.1 jit_solution(958596732300745677)
XLA Ops:
  0.6 72.3 %shard_map.101 = (f32[256,128]{1,0:T(8,128)S(1)}, f32[256,128]{1,0:T(8,128)S(1)}, f32[256,512]{1,0:T(8,128)S(1)}, f32[256,512]{1,0:T(8,128)S(1)}, f32[1,256]{1,0:T(1,128)S(1)}) custom-call(f32[256,512]{1,0:T(8,128)} %res_re.1, f32[256,512]{1,0:T(8,128)} %res_im.1, f32[256,512]{1,0:T(8,128)} %basis_re.1, f32[256,512]{1,0:T(8,128)} %basis_im.1, ...), custom_call_target="tpu_custom_call" | custom-call | tf_op jit(solution)/shard_map/pallas_call | solution.py:480
  73.0 1.1 %shard_map.102 = (f32[256,128]{1,0:T(8,128)}, f32[256,128]{1,0:T(8,128)}, f32[256,512]{1,0:T(8,128)}, f32[256,512]{1,0:T(8,128)}, f32[1,256]{1,0:T(1,128)}) custom-call(f32[256,128]{1,0:T(8,128)S(1)} %get-tuple-element.15.refs_0_, f32[256,128]{1,0:T(8,128)S(1)} %get-tuple-element.16.refs_1_, f32[256,512]{1,0:T(8,128)S(1)} %get-tuple-element.17.refs_2_, ...), custom_call_target="tpu_custom_call" | custom-call | tf_op jit(solution)/shard_map/pallas_call | solution.py:488

commit v4 on v3

--- a/solution.py
+++ b/solution.py
@@ -71,10 +71,10 @@
     out_coef_re, out_coef_im, out_new_re, out_new_im, out_err,
     live, live_h, basis, base, vlen, vpiv, picked, far, relay, near, ysum, yr, kout, kin, pall, kall, wt,
     coef_re, coef_im, new_re, new_im, err,
-    xpart, xpair, xhalf, xin, xfull,
-    gpart, gpair, ghalf, gin, gfull, cpart, cpair, chalf, cin, cfull, dpart, dpair, dhalf, din, eout, ein,
-    in_s, rx_s, rx_r, ry_s, ry_r, k_s, k_r, p_s, p_r, py_s, py_r, px_s, px_r, pr_s, pr_r,
-    kg_s, kg_r, zs_s, zs_r, zg_s, zg_r, c_s, c_r, e_s, e_r, out_s,
+    xpart, xpair, xhalf, xin, xfull, gpart, gin, gfull, kspan,
+    cpart, cpair, chalf, cin, cfull, dpart, dpair, dhalf, din, eout, ein,
+    in_s, rf_s, rf_r, rn_s, rn_r, rr_s, rr_r, ry_s, ry_r, k_s, k_r, p_s, p_r, py_s, py_r, px_s, px_r, pr_s, pr_r,
+    kg_s, kg_r, zs_s, zs_r, zg_s, zg_r, c_s, c_r, g_s, g_r, e_s, e_r, out_s,
 ):
     nx, ny, nz, nc = torus
     x, y, z, c = (lax.axis_index(a) for a in AXES)
@@ -112,6 +112,7 @@
         pl.semaphore_signal(barrier, inc=1, device_id=peer, device_id_type=pl.DeviceIdType.MESH)
 
     started = []
+    to_right, to_left = (right, y, z, c), (left, y, z, c)
 
     def push(src, dst, send, recv, to):
         copy = pltpu.make_async_remote_copy(
@@ -125,6 +126,21 @@
     def arrived(copies):
         for copy in copies:
             copy.wait_recv()
+
+    finals = []
+
+    def fan(pairs, send, recv, extent):
+        for src, dst, to in pairs:
+            pltpu.make_async_remote_copy(
+                src_ref=src, dst_ref=dst, send_sem=send, recv_sem=recv, device_id=to,
+                device_id_type=pl.DeviceIdType.MESH,
+            ).start()
+        whole = pltpu.make_async_remote_copy(
+            src_ref=extent, dst_ref=extent, send_sem=send, recv_sem=recv, device_id=to_right,
+            device_id_type=pl.DeviceIdType.MESH,
+        )
+        finals.append(whole)
+        return whole
 
     def chunk_of(i, size):
         return pl.ds(pl.multiple_of(i * size, size), size)
@@ -155,17 +171,16 @@
 
     pl.semaphore_wait(barrier, len(peers))
 
-    half = bins // 2
+    half, piece = bins // 2, span // 2
     ahead, behind = pl.ds(0, half), pl.ds(half, half)
-    to_right, to_left = (right, y, z, c), (left, y, z, c)
-    far_copies = [
-        push(picked.at[chunk_of(across, span), ahead], far.at[0], rx_s.at[0], rx_r.at[0], to_right),
-        push(picked.at[chunk_of(across, span), behind], far.at[1], rx_s.at[1], rx_r.at[1], to_left),
-    ]
-    near_copies = [
-        push(picked.at[chunk_of(right, span), behind], near.at[0, :, behind], rx_s.at[2], rx_r.at[2], to_right),
-        push(picked.at[chunk_of(left, span), ahead], near.at[1, :, ahead], rx_s.at[3], rx_r.at[3], to_left),
-    ]
+    ways = ((to_right, right, ahead), (to_left, left, behind))
+    far_copies = []
+    for i in range(2):
+        for k, (to, _, lanes) in enumerate(ways):
+            at = pl.ds(pl.multiple_of(across * span + i * piece, piece), piece)
+            far_copies.append(
+                push(picked.at[at, lanes], far.at[k, pl.ds(i * piece, piece)], rf_s.at[i, k], rf_r.at[i, k], to)
+            )
 
     for i, value in enumerate(halves(live[...])):
         live_h[i] = value
@@ -194,45 +209,53 @@
     def scatter(k, pair, part, got, summed, inward):
         arrived([pair])
         summed[...] = part[c] + got[...]
-        return [push(summed.at[p], inward.at[i], zs_s.at[k, i], zs_r.at[k, i], (x, y, p, c)) for i, p in zs]
+        return fan([(summed.at[p], inward.at[i], (x, y, p, c)) for i, p in zs], zs_s.at[k], zs_r.at[k], inward)
 
     def gathered(copies, summed, inward):
-        arrived(copies)
+        arrived([copies])
         total = summed[z]
         for i in range(nz - 1):
             total = total + inward[i]
         return total
 
-    def spread(k, total, full):
+    def spread(k, total, full, extent):
         full[c, z] = total
-        return [push(full.at[c, z], full.at[c, z], zg_s.at[k, i], zg_r.at[k, i], (x, y, p, c)) for i, p in zs]
+        at = full.at[c, z]
+        return fan([(at, at, (x, y, p, c)) for i, p in zs], zg_s.at[k], zg_r.at[k], extent)
 
     def share(k, copies, full):
-        arrived(copies)
+        arrived([copies])
         return push(full.at[c], full.at[c], c_s.at[k], c_r.at[k], (x, y, z, 1 - c))
 
+    near_started = [
+        (picked.at[chunk_of(next_x, span), other], near.at[k, :, other], to)
+        for k, ((to, next_x, _), other) in enumerate(zip(ways, (behind, ahead)))
+    ]
+    near_begun = fan(near_started, rn_s.at[0], rn_r.at[0], far)
     scatter_rows(xpart, both)
     x_pair = pair_up(0, xpart, xpair)
     turned_side = tuple(jnp.concatenate([-base[2 + i], base[i]], axis=1) for i in range(2))
     both = tuple(jnp.concatenate([right_side[i], turned_side[i]], axis=0) for i in range(2))
     scatter_rows(dpart, product((live_h[0], live_h[1]), both, NT))
     x_scatter = scatter(0, x_pair, xpart, xpair, xhalf, xin)
-    d_pair = pair_up(3, dpart, dpair)
-
-    arrived(far_copies[:1])
-    relay[0] = picked[chunk_of(right, span), :half] + far[0]
-    near_copies.append(push(relay.at[0], near.at[0, :, ahead], rx_s.at[4], rx_r.at[4], to_right))
-    arrived(far_copies[1:])
-    relay[1] = picked[chunk_of(left, span), half:] + far[1]
-    near_copies.append(push(relay.at[1], near.at[1, :, behind], rx_s.at[5], rx_r.at[5], to_left))
-    d_scatter = scatter(3, d_pair, dpart, dpair, dhalf, din)
-    arrived(near_copies)
+    d_pair = pair_up(2, dpart, dpair)
+
+    relays = []
+    for i in range(2):
+        for k, (to, next_x, lanes) in enumerate(ways):
+            arrived([far_copies[2 * i + k]])
+            at = pl.ds(pl.multiple_of(next_x * span + i * piece, piece), piece)
+            part = pl.ds(i * piece, piece)
+            relay[k, i * piece : (i + 1) * piece] = (
+                picked[at, k * half : (k + 1) * half] + far[k, i * piece : (i + 1) * piece]
+            )
+            relays.append(push(relay.at[k, part], near.at[k, part, lanes], rr_s.at[i, k], rr_r.at[i, k], to))
+    d_scatter = scatter(2, d_pair, dpart, dpair, dhalf, din)
+    arrived([near_begun, *relays])
     ysum[...] = picked[chunk_of(x, span), :] + near[0] + near[1]
-    y_copies = [
-        push(ysum.at[chunk_of(p, 8)], yr.at[i], ry_s.at[i], ry_r.at[i], (x, p, z, c)) for i, p in ys
-    ]
-    x_spread = spread(0, gathered(x_scatter, xhalf, xin), xfull)
-    arrived(y_copies)
+    y_copies = fan([(ysum.at[chunk_of(p, 8)], yr.at[i], (x, p, z, c)) for i, p in ys], ry_s.at[0], ry_r.at[0], yr)
+    x_spread = spread(0, gathered(x_scatter, xhalf, xin), xfull, xin)
+    arrived([y_copies])
     chunk = ysum[chunk_of(y, 8), :]
     for i in range(ny - 1):
         chunk = chunk + yr[i]
@@ -245,6 +268,8 @@
         yrecv, xrecv, rrecv = rs
         lanes = (pl.ds(0, wide // 2), pl.ds(wide // 2, wide // 2))
         copies = {}
+
+        extents = []
 
         def rows_of(i, d):
             return pl.ds(pl.multiple_of((i * ny + lax.rem(y + ny - d, ny)) * 8, 8), 8)
@@ -281,21 +306,20 @@
     sign_k = jnp.where(lax.broadcasted_iota(jnp.int32, (8, nb), 0) < 4, 1.0, -1.0).astype(F32)
     a, b = short_product(chunk, (b_re, b_im), NT)
     kout[...] = a + sign_k * pltpu.roll(b, 4, 0)
-    k_copies = [push(kout, kin.at[i], k_s.at[i], k_r.at[i], to) for i, to in fs]
-    x_last = share(0, x_spread, xfull)
+    k_copies = fan([(kout, kin.at[i], to) for i, to in fs], k_s.at[0], k_r.at[0], kin)
     for d in order:
         p_x(d)
     late = [0] + order
     early, late = late[:3], late[3:]
     for d in early:
         p_further(d)
-    arrived(k_copies)
+    arrived([k_copies])
     proj = kout[...]
     for i in range(len(fs)):
         proj = proj + kin[i]
     at = chunk_of(mine, 8)
     kall[at, :] = proj
-    k_gather = [push(kall.at[at], kall.at[at], kg_s.at[i], kg_r.at[i], to) for i, to in plane]
+    k_gather = fan([(kall.at[at], kall.at[at], to) for i, to in plane], kg_s.at[0], kg_r.at[0], kspan)
     for d in late:
         p_further(d)
     p_finish()
@@ -318,15 +342,23 @@
     take_imag = (from_row == real_row + 4).astype(F32).astype(BF16)
     w = (wt[0], wt[1])
     top = tuple(dot(take_real, part, NN).astype(BF16) for part in w)
-    scatter_rows(gpart, product(top, w, NT))
-    g_pair = pair_up(1, gpart, gpair)
+    gram = product(top, w, NT)
+    for i in range(nz * nc):
+        gpart[i] = gram[i * gpart.shape[1] : (i + 1) * gpart.shape[1]]
+    g_scatter = fan([(gpart.at[to[2] * nc + to[3]], gin.at[i], to) for i, to in fs], g_s.at[0], g_r.at[0], gin)
+    x_last = share(0, x_spread, xfull)
     scatter_rows(cpart, product((live_h[0], live_h[1]), w, NT))
-    c_pair = pair_up(2, cpart, cpair)
-
-    g_scatter = scatter(1, g_pair, gpart, gpair, ghalf, gin)
-    c_scatter = scatter(2, c_pair, cpart, cpair, chalf, cin)
+    c_pair = pair_up(1, cpart, cpair)
+
+    c_scatter = scatter(1, c_pair, cpart, cpair, chalf, cin)
+    arrived([g_scatter])
+    total = gpart[f]
+    for i in range(len(fs)):
+        total = total + gin[i]
+    gfull[f] = total
+    g_gather = fan([(gfull.at[f], gfull.at[f], to) for _, to in fs], g_s.at[1], g_r.at[1], gin)
     arrived([x_last])
-    arrived(k_gather)
+    arrived([k_gather])
 
     inner = halves(xfull[...].reshape(nb, nb))
 
@@ -340,17 +372,15 @@
     k_both = both_parts(kall[...], sign_all, part_all)
     t_both = both_parts(taken, sign_all, part_all)
     less = product(t_both, k_both, NT) + product(rest, t_both, NT)
-    g_spread = spread(1, gathered(g_scatter, ghalf, gin), gfull)
     kept = gathered(d_scatter, dhalf, din)
     total = gathered(c_scatter, chalf, cin)
-    c_spread = spread(2, total - product(halves(kept), t_both, NT), cfull)
+    c_spread = spread(1, total - product(halves(kept), t_both, NT), cfull, cin)
     taken = halves(taken)
     back = product(taken, b_re, NN) - sign * swapped(product(taken, b_im, NN), is_im, 0)
     for i, value in enumerate(both_parts(pall[...] - back, sign, is_im)):
         wt[i] = value
     w = (wt[0], wt[1])
-    g_last = share(1, g_spread, gfull)
-    arrived([g_last])
+    arrived([g_gather])
 
     gram = gfull[...].reshape(npiv, emb)
     col_part = lax.rem(lax.broadcasted_iota(jnp.int32, (npiv, emb), 1), 8) // 4
@@ -369,7 +399,7 @@
     zed = None
     for step in range(NS_STEPS):
         if step == 3:
-            c_last = share(2, c_spread, cfull)
+            c_last = share(1, c_spread, cfull)
         yh = halves(your)
         mix = your if zed is None else product(halves(zed), yh, NN)
         s = 1.5 * ident - 0.5 * mix
@@ -380,19 +410,18 @@
     zed = zed * (1.0 / jnp.sqrt(bound))
 
     zed_out = tuple(dot(place, part, NN).astype(BF16) for part in halves(zed))
-    block = product(halves((zed_out[0].astype(F32) + zed_out[1].astype(F32)) * scale_row), w, NN)
-    block = halves(block)
     arrived([c_last])
     cross = cfull[...].reshape(rows, emb)
     coef = product(halves(cross * scale_row), zed_out, NT)
     coef_re[...] = coef[:, :npiv]
     coef_im[...] = coef[:, npiv:]
+    weights = halves((zed_out[0].astype(F32) + zed_out[1].astype(F32)) * scale_row)
+    back = product(halves(product(halves(coef), weights, NN)), w, NN)
     sums = []
     for part in blocks:
         mask = mask_of(part)
-        back = product(halves(coef[part, :]), block, NN)
-        real = (live[part, :bins] - back[:, :bins]) * mask
-        imag = (live[part, bins:] - back[:, bins:]) * mask
+        real = (live[part, :bins] - back[part, :bins]) * mask
+        imag = (live[part, bins:] - back[part, bins:]) * mask
         new_re[part, :] = real
         new_im[part, :] = imag
         square = real * real + imag * imag
@@ -401,19 +430,19 @@
     summed = sum(dot(ones, part, NT) for part in thirds(jnp.concatenate(sums, axis=0)))
     eout[...] = summed[0:1, :]
     ein[f] = summed[0:1, :]
-    copies = [push(eout, ein.at[f], e_s.at[i], e_r.at[i], to) for i, to in fs]
+    e_copies = fan([(eout, ein.at[f], to) for _, to in fs], e_s.at[0], e_r.at[0], ein.at[pl.ds(0, len(fs))])
     results = [(coef_re, out_coef_re), (coef_im, out_coef_im), (new_re, out_new_re), (new_im, out_new_im), (err, out_err)]
     results = [pltpu.make_async_copy(src, dst, out_s.at[i]) for i, (src, dst) in enumerate(results)]
     for result in results[:4]:
         result.start()
-    arrived(copies)
+    arrived([e_copies])
     total = ein[0]
     for i in range(1, nz * nc):
         total = total + ein[i]
     err[...] = total / (BIN_BLOCK * vlen[...]).astype(F32)
     results[4].start()
 
-    for copy in started:
+    for copy in started + finals:
         copy.wait_send()
     for result in results:
         result.wait()
@@ -464,16 +493,16 @@
         vmem((2, emb, 2 * bins), BF16),
         *[vmem(shape, F32) for shape in shapes],
         *summed(nb, nb),
-        *summed(emb // 2, emb),
+        vmem((nf, emb // 2 // nf, emb), F32), vmem((nf - 1, emb // 2 // nf, emb), F32), vmem((nf, emb // 2 // nf, emb), F32),
+        vmem((nx * ny - 1, 8, nb), F32),
         *summed(rows, emb),
         *summed(rows, 2 * nb)[:4],
         vmem((1, rows), F32), vmem((nf, 1, rows), F32),
-        dma((6,)), dma((6,)), dma((6,)), dma((ny - 1,)), dma((ny - 1,)), dma((nf - 1,)), dma((nf - 1,)),
-        dma((4,)), dma((4,)),
-        dma((ny - 1,)), dma((ny - 1,)), dma((ny, 2)), dma((ny, 2)), dma((ny, 2)), dma((ny, 2)),
-        dma((nx * ny - 1,)), dma((nx * ny - 1,)),
-        dma((4, nz - 1)), dma((4, nz - 1)), dma((3, nz - 1)), dma((3, nz - 1)), dma((3,)), dma((3,)),
-        dma((nf - 1,)), dma((nf - 1,)), dma((5,)),
+        dma((6,)),
+        *[dma((2, 2))] * 2, *[dma((1,))] * 2, *[dma((2, 2))] * 2, *[dma((1,))] * 2, *[dma((1,))] * 2, *[dma((3,))] * 2,
+        *[dma((ny - 1,))] * 2, *[dma((ny, 2))] * 4,
+        *[dma((1,))] * 2, *[dma((3,))] * 2, *[dma((2,))] * 2, *[dma((2,))] * 2, *[dma((2,))] * 2, *[dma((1,))] * 2,
+        dma((5,)),
     ]
     here = pl.BlockSpec(memory_space=pltpu.VMEM)
     there = pl.BlockSpec(memory_space=pl.ANY)

time: 74.2 us -> 69.5 us (0.937)
  Pallas kernels: 73.4 us -> 68.7 us
    pallas_call x1, Pallas kernels: 72.3 us -> 67.6 us  [body(): pl.pallas_call(functools.partial(kernel, torus), out_shape=[vmem(shape, F...]
where the time goes in v4:
time: 69.5 us; the launch traced here: 69.4 us
  Pallas kernels  68.7 us (99%)
    pallas_call x1, Pallas kernels, body(): pl.pallas_call(functools.partial(kernel, torus), out_shape=[vmem(shape, F...  67.6 us

profile of v4, /device:TPU:1, one launch (start us, length us, event | category | flops | bytes accessed | tf_op | source)
XLA Modules:
  0.0 69.4 jit_solution(18076816006925258036)
XLA Ops:
  0.6 67.6 %shard_map.101 = (f32[256,128]{1,0:T(8,128)S(1)}, f32[256,128]{1,0:T(8,128)S(1)}, f32[256,512]{1,0:T(8,128)S(1)}, f32[256,512]{1,0:T(8,128)S(1)}, f32[1,256]{1,0:T(1,128)S(1)}) custom-call(f32[256,512]{1,0:T(8,128)} %res_re.1, f32[256,512]{1,0:T(8,128)} %res_im.1, f32[256,512]{1,0:T(8,128)} %basis_re.1, f32[256,512]{1,0:T(8,128)} %basis_im.1, ...), custom_call_target="tpu_custom_call" | custom-call | tf_op jit(solution)/shard_map/pallas_call | solution.py:509
  68.3 1.1 %shard_map.102 = (f32[256,128]{1,0:T(8,128)}, f32[256,128]{1,0:T(8,128)}, f32[256,512]{1,0:T(8,128)}, f32[256,512]{1,0:T(8,128)}, f32[1,256]{1,0:T(1,128)}) custom-call(f32[256,128]{1,0:T(8,128)S(1)} %get-tuple-element.15.refs_0_, f32[256,128]{1,0:T(8,128)S(1)} %get-tuple-element.16.refs_1_, f32[256,512]{1,0:T(8,128)S(1)} %get-tuple-element.17.refs_2_, ...), custom_call_target="tpu_custom_call" | custom-call | tf_op jit(solution)/shard_map/pallas_call | solution.py:517

commit v5 on v4

v5 whole, which is shorter than its diff:
```python
import functools

import jax
import jax.numpy as jnp
from jax import lax
from jax.experimental import pallas as pl
from jax.experimental.pallas import tpu as pltpu
from jax.sharding import Mesh
from jax.sharding import PartitionSpec as P

BIN_BLOCK = 128
NS_STEPS = 6
EPSILON = 1e-06
TORUS = (4, 8, 8, 2)
AXES = ("x", "y", "z", "core")
F32 = jnp.float32
BF16 = jnp.bfloat16


def dot(left, right, dims):
    return lax.dot_general(left, right, (dims, ((), ())), preferred_element_type=F32)


NN = ((1,), (0,))
NT = ((1,), (1,))


def halves(a):
    high = a.astype(BF16)
    return high, (a - high.astype(F32)).astype(BF16)


def thirds(a):
    high = a.astype(BF16)
    rest = a - high.astype(F32)
    mid = rest.astype(BF16)
    return high, mid, (rest - mid.astype(F32)).astype(BF16)


def product(left, right, dims):
    lh, ll = left
    rh, rl = right
    along = dims[1][0]
    return dot(jnp.concatenate([lh, ll, lh], axis=1), jnp.concatenate([rh, rh, rl], axis=along), dims)


def chosen(select, a):
    parts = thirds(a)
    return dot(jnp.concatenate([select] * 3, axis=1), jnp.concatenate(parts, axis=0), NN)


def embedded(row):
    n = row.shape[1] // 2
    return jnp.concatenate([row, jnp.concatenate([-row[:, n:], row[:, :n]], axis=1)], axis=0)


def crossed(a, b):
    n = a.shape[0] // 2
    return jnp.concatenate([a[:n] - b[n:], a[n:] + b[:n]], axis=0)


def as_rows(a):
    n = a.shape[0] // 2
    return jnp.concatenate([a[:n], a[n:]], axis=1)


def short_product(chunk, rights, dims):
    high = chunk.astype(BF16).astype(F32)
    both = jnp.concatenate([high, chunk - high], axis=0).astype(BF16)
    out = []
    for rh, rl in rights:
        a = dot(both, rh, dims)
        b = dot(both, rl, dims)
        out.append((a[:8] + a[8:]) + (b[:8] + b[8:]))
    return out


def kernel(
    torus,
    res_re, res_im, basis_re, basis_im, lens, piv,
    out_coef_re, out_coef_im, out_new_re, out_new_im, out_err,
    live, live_h, basis, base, vlen, vpiv, picked, xr, ysum, yr, kout, kin, pall, kall, wt,
    coef_re, coef_im, new_re, new_im, err,
    xpart, xpair, xhalf, xin, xfull, gpart, gin, gfull, kspan,
    cpart, cpair, chalf, cin, cfull, dpart, dpair, dhalf, din, eout, ein,
    in_s, rx_s, rx_r, ry_s, ry_r, k_s, k_r, p_s, p_r, py_s, py_r, px_s, px_r, ky_s, ky_r, kx_s, kx_r,
    zs_s, zs_r, zg_s, zg_r, c_s, c_r, g_s, g_r, e_s, e_r, out_s,
):
    nx, ny, nz, nc = torus
    x, y, z, c = (lax.axis_index(a) for a in AXES)
    f = z * nc + c
    rows, bins = res_re.shape
    emb = 8 * nx * ny
    npiv = emb // 2
    nb = basis_re.shape[0]
    span = 8 * ny

    def hops(d, n):
        return min(d, n - d)

    xs = [(d - 1, lax.rem(x + d, nx)) for d in sorted(range(1, nx), key=lambda d: -hops(d, nx))]
    ys = [(d - 1, lax.rem(y + d, ny)) for d in sorted(range(1, ny), key=lambda d: -hops(d, ny))]
    zs = [(d - 1, lax.rem(z + d, nz)) for d in sorted(range(1, nz), key=lambda d: -hops(d, nz))]
    fs = sorted(((dz, dc) for dz in range(nz) for dc in range(nc) if dz or dc), key=lambda d: -hops(d[0], nz))
    fs = [(dz * nc + dc - 1, (x, y, lax.rem(z + dz, nz), lax.rem(c + dc, nc))) for dz, dc in fs]
    barrier = pltpu.get_barrier_semaphore()
    peers = [to for _, to in fs] + [(x, p, z, c) for _, p in ys] + [(p, y, z, c) for _, p in xs]
    for peer in peers:
        pl.semaphore_signal(barrier, inc=1, device_id=peer, device_id_type=pl.DeviceIdType.MESH)
    loads = [(lens, vlen), (piv, vpiv), (res_re, live.at[:, pl.ds(0, bins)]), (res_im, live.at[:, pl.ds(bins, bins)])]
    loads += [(basis_re, basis.at[0]), (basis_im, basis.at[1])]
    loads = [pltpu.make_async_copy(src, dst, in_s.at[i]) for i, (src, dst) in enumerate(loads)]
    for load in loads:
        load.start()

    started = []
    anyone = fs[0][1]

    def described(src, dst, send, recv, to):
        return pltpu.make_async_remote_copy(
            src_ref=src, dst_ref=dst, send_sem=send, recv_sem=recv, device_id=to,
            device_id_type=pl.DeviceIdType.MESH,
        )

    def begin(src, dst, send, recv, to):
        copy = described(src, dst, send, recv, to)
        copy.start()
        return copy

    def push(src, dst, send, recv, to):
        copy = begin(src, dst, send, recv, to)
        started.append(copy)
        return copy

    def arrived(copies):
        for copy in copies:
            copy.wait_recv()

    finals = []

    def fan(pairs, send, recv, extent):
        for src, dst, to in pairs:
            begin(src, dst, send, recv, to)
        whole = described(extent, extent, send, recv, anyone)
        finals.append(whole)
        return whole

    def chunk_of(i, size):
        return pl.ds(pl.multiple_of(i * size, size), size)

    for load in loads[:4]:
        load.wait()
    diagonal = lax.broadcasted_iota(jnp.int32, (rows, rows), 0) == lax.broadcasted_iota(jnp.int32, (rows, rows), 1)
    ends = jnp.sum(jnp.where(diagonal, vlen[...] * BIN_BLOCK, 0).astype(F32), axis=1, keepdims=True)
    first_bin = f * bins

    def mask_of(part):
        count = part.stop - part.start
        at = first_bin + lax.broadcasted_iota(jnp.int32, (count, bins), 1)
        return (at.astype(F32) < ends[part, :]).astype(F32)

    blocks = [slice(r, min(r + 64, rows)) for r in range(0, rows, 64)]
    for part in blocks:
        mask = mask_of(part)
        live[part, :bins] = live[part, :bins] * mask
        live[part, bins:] = live[part, bins:] * mask
    to_row = lax.broadcasted_iota(jnp.int32, (emb, npiv), 0)
    of_row = lax.broadcasted_iota(jnp.int32, (emb, npiv), 1) == lax.rem(to_row, 4) * (nx * ny) + to_row // 8
    wanted = jnp.sum(jnp.where(of_row, vpiv[...], 0).astype(F32), axis=1, keepdims=True)
    own = (x * ny + y) * rows + lax.broadcasted_iota(jnp.int32, (emb, rows), 1)
    select = (wanted == own.astype(F32)).astype(F32).astype(BF16)
    is_im = lax.rem(lax.broadcasted_iota(jnp.int32, (emb, bins), 0), 8) // 4
    picked[...] = jnp.where(is_im == 0, chosen(select, live[:, :bins]), chosen(select, live[:, bins:]))

    pl.semaphore_wait(barrier, len(peers))

    x_copies = fan([(picked.at[chunk_of(p, span)], xr.at[i], (p, y, z, c)) for i, p in xs], rx_s.at[0], rx_r.at[0], xr)

    for i, value in enumerate(halves(live[...])):
        live_h[i] = value
    for load in loads[4:]:
        load.wait()
    for i in range(2):
        high, low = halves(basis[i])
        base[2 * i] = high
        base[2 * i + 1] = low
    b_re = (base[0], base[1])
    b_im = (base[2], base[3])
    plus = jnp.concatenate([basis[0] + basis[1], basis[1] - basis[0]], axis=1)
    right_side = tuple(jnp.concatenate([base[i], base[2 + i]], axis=1) for i in range(2))
    both = product(halves(plus), right_side, NT)

    def scatter_rows(part, value):
        size = part.shape[2]
        for i in range(nc):
            for j in range(nz):
                at = (i * nz + j) * size
                part[i, j] = value[at : at + size]

    def pair_up(k, part, got):
        return push(part.at[1 - c], got, p_s.at[k], p_r.at[k], (x, y, z, 1 - c))

    def scatter(k, pair, part, got, summed, inward):
        arrived([pair])
        summed[...] = part[c] + got[...]
        return fan([(summed.at[p], inward.at[i], (x, y, p, c)) for i, p in zs], zs_s.at[k], zs_r.at[k], inward)

    def gathered(copies, summed, inward):
        arrived([copies])
        total = summed[z]
        for i in range(nz - 1):
            total = total + inward[i]
        return total

    def spread(k, total, full, extent):
        full[c, z] = total
        at = full.at[c, z]
        return fan([(at, at, (x, y, p, c)) for i, p in zs], zg_s.at[k], zg_r.at[k], extent)

    def share(k, copies, full):
        arrived([copies])
        return push(full.at[c], full.at[c], c_s.at[k], c_r.at[k], (x, y, z, 1 - c))

    scatter_rows(xpart, both)
    x_pair = pair_up(0, xpart, xpair)
    turned_side = tuple(jnp.concatenate([-base[2 + i], base[i]], axis=1) for i in range(2))
    both = tuple(jnp.concatenate([right_side[i], turned_side[i]], axis=0) for i in range(2))
    scatter_rows(dpart, product((live_h[0], live_h[1]), both, NT))
    x_scatter = scatter(0, x_pair, xpart, xpair, xhalf, xin)
    d_pair = pair_up(2, dpart, dpair)

    d_scatter = scatter(2, d_pair, dpart, dpair, dhalf, din)
    arrived([x_copies])
    total = picked[chunk_of(x, span), :]
    for i in range(nx - 1):
        total = total + xr[i]
    ysum[...] = total
    y_copies = fan([(ysum.at[chunk_of(p, 8)], yr.at[i], (x, p, z, c)) for i, p in ys], ry_s.at[0], ry_r.at[0], yr)
    arrived([y_copies])
    chunk = ysum[chunk_of(y, 8), :]
    for i in range(ny - 1):
        chunk = chunk + yr[i]

    mine = x * ny + y
    order = sorted(range(1, ny), key=lambda d: min(d, ny - d))


    def gather(buf, sems, y_extent, x_extent):
        ysend, yrecv, xsend, xrecv = sems

        def rows_of(d):
            return buf.at[pl.ds(pl.multiple_of((x * ny + lax.rem(y + ny - d, ny)) * 8, 8), 8)]

        own_rows = rows_of(0)
        along_y = {
            i + 1: begin(own_rows, own_rows, ysend.at[0], yrecv.at[i], (x, p, z, c)) for i, p in ys
        }

        def forward(d):
            if d:
                arrived([along_y[d]])
            for _, p in xs:
                begin(rows_of(d), rows_of(d), xsend.at[0], xrecv.at[0], (p, y, z, c))

        forward(0)
        last = described(x_extent, x_extent, xsend.at[0], xrecv.at[0], anyone)
        finals.extend([described(y_extent, y_extent, ysend.at[0], yrecv.at[0], anyone), last])
        return forward, last

    pall[chunk_of(mine, 8), :] = chunk
    p_forward, p_last = gather(pall, (py_s, py_r, px_s, px_r), yr, xr)
    sign_k = jnp.where(lax.broadcasted_iota(jnp.int32, (8, nb), 0) < 4, 1.0, -1.0).astype(F32)
    a, b = short_product(chunk, (b_re, b_im), NT)
    kout[...] = a + sign_k * pltpu.roll(b, 4, 0)
    k_copies = fan([(kout, kin.at[i], to) for i, to in fs], k_s.at[0], k_r.at[0], kin)
    for d in order:
        p_forward(d)
    arrived([k_copies])
    proj = kout[...]
    for i in range(len(fs)):
        proj = proj + kin[i]
    kall[chunk_of(mine, 8), :] = proj
    k_forward, k_last = gather(kall, (ky_s, ky_r, kx_s, kx_r), kin.at[pl.ds(0, ny - 1)], kspan)
    x_spread = spread(0, gathered(x_scatter, xhalf, xin), xfull, xin)
    arrived([p_last])

    def set_block(rows_by_part):
        top = as_rows(rows_by_part)
        n = top.shape[1] // 2
        bottom = jnp.concatenate([-top[:, n:], top[:, :n]], axis=1)
        for i, (above, below) in enumerate(zip(halves(top), halves(bottom))):
            wt[i, :npiv] = above
            wt[i, npiv:] = below
        return top, bottom

    to_row = lax.broadcasted_iota(jnp.int32, (emb, emb), 0)
    from_row = lax.broadcasted_iota(jnp.int32, (emb, emb), 1)
    by_part = (from_row == lax.rem(to_row, nx * ny) * 8 + to_row // (nx * ny)).astype(F32).astype(BF16)
    pivots = chosen(by_part, pall[...])
    top, bottom = set_block(pivots)
    gram = product((wt[0, :npiv], wt[1, :npiv]), halves(top + bottom), NT)
    for i in range(nz * nc):
        gpart[i] = gram[i * gpart.shape[1] : (i + 1) * gpart.shape[1]]
    g_scatter = fan([(gpart.at[to[2] * nc + to[3]], gin.at[i], to) for i, to in fs], g_s.at[0], g_r.at[0], gin)
    for d in order:
        k_forward(d)
    scatter_rows(cpart, product((live_h[0], live_h[1]), (wt[0], wt[1]), NT))
    c_pair = pair_up(1, cpart, cpair)

    c_scatter = scatter(1, c_pair, cpart, cpair, chalf, cin)
    arrived([g_scatter])
    total = gpart[f]
    for i in range(len(fs)):
        total = total + gin[i]
    gfull[f] = total
    g_gather = fan([(gfull.at[f], gfull.at[f], to) for _, to in fs], g_s.at[1], g_r.at[1], gin)
    x_last = share(0, x_spread, xfull)
    arrived([x_last])
    arrived([k_last])

    inner = halves(xfull[...].reshape(nb, nb))

    def times_inner(a):
        both = halves(a)
        straight, across = product(both, inner, NN), product(both, inner, NT)
        return crossed(0.5 * (straight + across), 0.5 * (straight - across))

    def split_rows(a):
        parts = halves(as_rows(a))
        return parts, tuple(embedded(part) for part in parts)

    proj = chosen(by_part, kall[...])
    taken = 2.0 * proj - times_inner(proj)
    rest, _ = split_rows(proj - times_inner(taken))
    _, k_both = split_rows(proj)
    t_rows, t_both = split_rows(taken)
    less = product(t_rows, k_both, NT) + product(rest, t_both, NT)
    kept = gathered(d_scatter, dhalf, din)
    total = gathered(c_scatter, chalf, cin)
    c_spread = spread(1, total - product(halves(kept), t_both, NT), cfull, cin)
    taken = halves(taken)
    set_block(pivots - crossed(product(taken, b_re, NN), product(taken, b_im, NN)))
    w = (wt[0], wt[1])
    arrived([g_gather])

    gram = gfull[...].reshape(npiv, npiv)
    turned = gram.T
    gram = jnp.concatenate([0.5 * (gram + turned), 0.5 * (gram - turned)], axis=1) - less
    eye = lax.broadcasted_iota(jnp.int32, (npiv, emb), 0) == lax.broadcasted_iota(jnp.int32, (npiv, emb), 1)
    ident = eye.astype(F32)
    diag = gram * ident
    scale_col = 1.0 / jnp.sqrt(jnp.sum(diag, axis=1, keepdims=True) + EPSILON)
    scale_row = 1.0 / jnp.sqrt(jnp.sum(diag[:, :npiv], axis=0, keepdims=True) + EPSILON)
    scale_row = jnp.concatenate([scale_row, scale_row], axis=1)
    gram = gram * (scale_col * scale_row)
    bound = jnp.max(jnp.sum(jnp.abs(gram), axis=1, keepdims=True), axis=0, keepdims=True)
    your = gram / bound
    zed = None

    def times(left, right):
        return product(left, tuple(embedded(part) for part in right), NN)

    for step in range(NS_STEPS):
        if step == 3:
            c_last = share(1, c_spread, cfull)
        yh = halves(your)
        mix = your if zed is None else times(zh, yh)
        s = 1.5 * ident - 0.5 * mix
        sh = halves(s)
        if step < NS_STEPS - 1:
            your = times(yh, sh)
        zed = s if zed is None else times(sh, zh)
        zh = halves(zed)
    zed = zed * (1.0 / jnp.sqrt(bound))

    zed_e = tuple(embedded(part) for part in halves(zed))
    arrived([c_last])
    cross = cfull[...].reshape(rows, emb)
    coef = product(halves(cross * scale_row), zed_e, NT)
    coef_re[...] = coef[:, :npiv]
    coef_im[...] = coef[:, npiv:]
    back = product(halves(product(halves(coef), zed_e, NN) * scale_row), w, NN)
    sums = []
    for part in blocks:
        mask = mask_of(part)
        real = (live[part, :bins] - back[part, :bins]) * mask
        imag = (live[part, bins:] - back[part, bins:]) * mask
        new_re[part, :] = real
        new_im[part, :] = imag
        square = real * real + imag * imag
        sums.append(sum(square[:, i : i + 128] for i in range(0, bins, 128)))
    ones = jnp.ones((8, 128), BF16)
    summed = sum(dot(ones, part, NT) for part in thirds(jnp.concatenate(sums, axis=0)))
    eout[...] = summed[0:1, :]
    ein[f] = summed[0:1, :]
    e_copies = fan([(eout, ein.at[f], to) for _, to in fs], e_s.at[0], e_r.at[0], ein.at[pl.ds(0, len(fs))])
    results = [(coef_re, out_coef_re), (coef_im, out_coef_im), (new_re, out_new_re), (new_im, out_new_im), (err, out_err)]
    results = [pltpu.make_async_copy(src, dst, out_s.at[i]) for i, (src, dst) in enumerate(results)]
    for result in results[:4]:
        result.start()
    arrived([e_copies])
    total = ein[0]
    for i in range(1, nz * nc):
        total = total + ein[i]
    err[...] = total / (BIN_BLOCK * vlen[...]).astype(F32)
    results[4].start()

    for copy in started + finals:
        copy.wait_send()
    for result in results:
        result.wait()


def handed_out(*refs):
    count = len(refs) // 2
    copies = [pltpu.make_async_copy(refs[i], refs[count + i], refs[-1].at[i]) for i in range(count)]
    for copy in copies:
        copy.start()
    for copy in copies:
        copy.wait()


def body(torus, res_re, res_im, basis_re, basis_im, lengths, pivots):
    nx, ny, nz, nc = torus
    rows, bins = res_re.shape
    nb = basis_re.shape[0]
    emb = 8 * nx * ny
    nf = nz * nc
    span = 8 * ny
    vmem = pltpu.VMEM
    dma = pltpu.SemaphoreType.DMA
    shapes = [(rows, emb // 2), (rows, emb // 2), (rows, bins), (rows, bins), (1, rows)]

    def summed(count, width):
        part = count // nf
        whole, across = vmem((nc, nz, part, width), F32), vmem((nz, part, width), F32)
        return [whole, across, across, vmem((nz - 1, part, width), F32), whole]

    scratch = [
        vmem((rows, 2 * bins), F32),
        vmem((2, rows, 2 * bins), BF16),
        vmem((2, nb, bins), F32),
        vmem((4, nb, bins), BF16),
        vmem((1, rows), jnp.int32),
        vmem((1, emb // 2), jnp.int32),
        vmem((emb, bins), F32),
        vmem((nx - 1, span, bins), F32),
        vmem((span, bins), F32),
        vmem((ny - 1, 8, bins), F32),
        vmem((8, nb), F32),
        vmem((nf - 1, 8, nb), F32),
        vmem((emb, bins), F32),
        vmem((emb, nb), F32),
        vmem((2, emb, 2 * bins), BF16),
        *[vmem(shape, F32) for shape in shapes],
        *summed(nb, nb),
        *[vmem((count, emb // 2 // nf, emb // 2), F32) for count in (nf, nf - 1, nf)],
        vmem(((nx - 1) * ny, 8, nb), F32),
        *summed(rows, emb),
        *summed(rows, 2 * nb)[:4],
        vmem((1, rows), F32), vmem((nf, 1, rows), F32),
        dma((6,)),
        *[dma((1,))] * 6, *[dma((3,))] * 2,
        *[dma((1,)), dma((ny - 1,)), dma((1,)), dma((1,))] * 2,
        *[dma((3,))] * 2, *[dma((2,))] * 2, *[dma((2,))] * 2, *[dma((2,))] * 2, *[dma((1,))] * 2,
        dma((5,)),
    ]
    here = pl.BlockSpec(memory_space=pltpu.VMEM)
    there = pl.BlockSpec(memory_space=pl.ANY)
    results = pl.pallas_call(
        functools.partial(kernel, torus),
        out_shape=[vmem(shape, F32) for shape in shapes],
        in_specs=[there] * 6,
        out_specs=[there] * 5,
        scratch_shapes=scratch,
        compiler_params=pltpu.CompilerParams(collective_id=0, has_side_effects=True),
    )(res_re, res_im, basis_re, basis_im, lengths.reshape(1, rows), pivots.reshape(1, emb // 2))
    coef_re, coef_im, new_re, new_im, err = pl.pallas_call(
        handed_out,
        out_shape=[jax.ShapeDtypeStruct(shape, F32) for shape in shapes],
        in_specs=[here] * 5,
        out_specs=[there] * 5,
        scratch_shapes=[dma((5,))],
    )(*[pltpu.with_memory_space_constraint(result, pltpu.VMEM) for result in results])
    return coef_re, coef_im, new_re, new_im, err.reshape(rows)


def build(mesh, torus):
    axes = Mesh(mesh.devices.reshape(torus), AXES)
    wave, freq = ("x", "y"), ("z", "core")
    in_specs = (P(wave, freq), P(wave, freq), P(None, freq), P(None, freq), P(wave), P())
    out_specs = (P(wave, None), P(wave, None), P(wave, freq), P(wave, freq), P(wave))
    return jax.shard_map(
        functools.partial(body, torus), mesh=axes, in_specs=in_specs, out_specs=out_specs, check_vma=False
    )


def solution(mesh):
    return build(mesh, TORUS)
```

time: 69.5 us -> 65 us (0.935)
  Pallas kernels: 68.7 us -> 64.3 us
    pallas_call x1, Pallas kernels: 67.6 us -> 63.2 us  [body(): pl.pallas_call(functools.partial(kernel, torus), out_shape=[vmem(shape, F...]
where the time goes in v5:
time: 65 us; the launch traced here: 64.9 us
  Pallas kernels  64.3 us (99%)
    pallas_call x1, Pallas kernels, body(): pl.pallas_call(functools.partial(kernel, torus), out_shape=[vmem(shape, F...  63.2 us

profile of v5, /device:TPU:1, one launch (start us, length us, event | category | flops | bytes accessed | tf_op | source)
XLA Modules:
  0.0 64.9 jit_solution(13187051580628083836)
XLA Ops:
  0.6 63.2 %shard_map.101 = (f32[256,128]{1,0:T(8,128)S(1)}, f32[256,128]{1,0:T(8,128)S(1)}, f32[256,512]{1,0:T(8,128)S(1)}, f32[256,512]{1,0:T(8,128)S(1)}, f32[1,256]{1,0:T(1,128)S(1)}) custom-call(f32[256,512]{1,0:T(8,128)} %res_re.1, f32[256,512]{1,0:T(8,128)} %res_im.1, f32[256,512]{1,0:T(8,128)} %basis_re.1, f32[256,512]{1,0:T(8,128)} %basis_im.1, ...), custom_call_target="tpu_custom_call" | custom-call | tf_op jit(solution)/shard_map/pallas_call | solution.py:470
  63.8 1.1 %shard_map.102 = (f32[256,128]{1,0:T(8,128)}, f32[256,128]{1,0:T(8,128)}, f32[256,512]{1,0:T(8,128)}, f32[256,512]{1,0:T(8,128)}, f32[1,256]{1,0:T(1,128)}) custom-call(f32[256,128]{1,0:T(8,128)S(1)} %get-tuple-element.15.refs_0_, f32[256,128]{1,0:T(8,128)S(1)} %get-tuple-element.16.refs_1_, f32[256,512]{1,0:T(8,128)S(1)} %get-tuple-element.17.refs_2_, ...), custom_call_target="tpu_custom_call" | custom-call | tf_op jit(solution)/shard_map/pallas_call | solution.py:478

commit v6 on v5

--- a/solution.py
+++ b/solution.py
@@ -79,11 +79,11 @@
     torus,
     res_re, res_im, basis_re, basis_im, lens, piv,
     out_coef_re, out_coef_im, out_new_re, out_new_im, out_err,
-    live, live_h, basis, base, vlen, vpiv, picked, xr, ysum, yr, kout, kin, pall, kall, wt,
+    live, live_h, basis, base, vlen, vpiv, picked, far, relay, near, ysum, yr, kout, kin, pall, kall, wt,
     coef_re, coef_im, new_re, new_im, err,
     xpart, xpair, xhalf, xin, xfull, gpart, gin, gfull, kspan,
-    cpart, cpair, chalf, cin, cfull, dpart, dpair, dhalf, din, eout, ein,
-    in_s, rx_s, rx_r, ry_s, ry_r, k_s, k_r, p_s, p_r, py_s, py_r, px_s, px_r, ky_s, ky_r, kx_s, kx_r,
+    cpart, cpair, chalf, cin, cfull, dpart, dpair, dhalf, din, dfull, eout, ein,
+    in_s, rf_s, rf_r, rn_s, rn_r, rr_s, rr_r, ry_s, ry_r, k_s, k_r, p_s, p_r, py_s, py_r, px_s, px_r, ky_s, ky_r, kx_s, kx_r,
     zs_s, zs_r, zg_s, zg_r, c_s, c_r, g_s, g_r, e_s, e_r, out_s,
 ):
     nx, ny, nz, nc = torus
@@ -174,7 +174,17 @@
 
     pl.semaphore_wait(barrier, len(peers))
 
-    x_copies = fan([(picked.at[chunk_of(p, span)], xr.at[i], (p, y, z, c)) for i, p in xs], rx_s.at[0], rx_r.at[0], xr)
+    half, piece = bins // 2, span // 2
+    ahead, behind = pl.ds(0, half), pl.ds(half, half)
+    right, left, across = (lax.rem(x + d, nx) for d in (1, nx - 1, 2))
+    ways = (((right, y, z, c), right, ahead), ((left, y, z, c), left, behind))
+    far_copies = []
+    for i in range(2):
+        for k, (to, _, lanes) in enumerate(ways):
+            at = pl.ds(pl.multiple_of(across * span + i * piece, piece), piece)
+            far_copies.append(
+                push(picked.at[at, lanes], far.at[k, pl.ds(i * piece, piece)], rf_s.at[i, k], rf_r.at[i, k], to)
+            )
 
     for i, value in enumerate(halves(live[...])):
         live_h[i] = value
@@ -221,6 +231,11 @@
         arrived([copies])
         return push(full.at[c], full.at[c], c_s.at[k], c_r.at[k], (x, y, z, 1 - c))
 
+    near_started = [
+        (picked.at[chunk_of(next_x, span), other], near.at[k, :, other], to)
+        for k, ((to, next_x, _), other) in enumerate(zip(ways, (behind, ahead)))
+    ]
+    near_begun = fan(near_started, rn_s.at[0], rn_r.at[0], far)
     scatter_rows(xpart, both)
     x_pair = pair_up(0, xpart, xpair)
     turned_side = tuple(jnp.concatenate([-base[2 + i], base[i]], axis=1) for i in range(2))
@@ -229,12 +244,19 @@
     x_scatter = scatter(0, x_pair, xpart, xpair, xhalf, xin)
     d_pair = pair_up(2, dpart, dpair)
 
+    relays = []
+    for i in range(2):
+        for k, (to, next_x, lanes) in enumerate(ways):
+            arrived([far_copies[2 * i + k]])
+            at = pl.ds(pl.multiple_of(next_x * span + i * piece, piece), piece)
+            part = pl.ds(i * piece, piece)
+            relay[k, i * piece : (i + 1) * piece] = (
+                picked[at, k * half : (k + 1) * half] + far[k, i * piece : (i + 1) * piece]
+            )
+            relays.append(push(relay.at[k, part], near.at[k, part, lanes], rr_s.at[i, k], rr_r.at[i, k], to))
     d_scatter = scatter(2, d_pair, dpart, dpair, dhalf, din)
-    arrived([x_copies])
-    total = picked[chunk_of(x, span), :]
-    for i in range(nx - 1):
-        total = total + xr[i]
-    ysum[...] = total
+    arrived([near_begun, *relays])
+    ysum[...] = picked[chunk_of(x, span), :] + near[0] + near[1]
     y_copies = fan([(ysum.at[chunk_of(p, 8)], yr.at[i], (x, p, z, c)) for i, p in ys], ry_s.at[0], ry_r.at[0], yr)
     arrived([y_copies])
     chunk = ysum[chunk_of(y, 8), :]
@@ -268,44 +290,47 @@
         return forward, last
 
     pall[chunk_of(mine, 8), :] = chunk
-    p_forward, p_last = gather(pall, (py_s, py_r, px_s, px_r), yr, xr)
+    p_forward, p_last = gather(pall, (py_s, py_r, px_s, px_r), yr, picked.at[pl.ds(0, (nx - 1) * span)])
     sign_k = jnp.where(lax.broadcasted_iota(jnp.int32, (8, nb), 0) < 4, 1.0, -1.0).astype(F32)
     a, b = short_product(chunk, (b_re, b_im), NT)
     kout[...] = a + sign_k * pltpu.roll(b, 4, 0)
     k_copies = fan([(kout, kin.at[i], to) for i, to in fs], k_s.at[0], k_r.at[0], kin)
     for d in order:
         p_forward(d)
+    x_spread = spread(0, gathered(x_scatter, xhalf, xin), xfull, xin)
+    d_spread = spread(2, gathered(d_scatter, dhalf, din), dfull, din)
     arrived([k_copies])
     proj = kout[...]
     for i in range(len(fs)):
         proj = proj + kin[i]
     kall[chunk_of(mine, 8), :] = proj
     k_forward, k_last = gather(kall, (ky_s, ky_r, kx_s, kx_r), kin.at[pl.ds(0, ny - 1)], kspan)
-    x_spread = spread(0, gathered(x_scatter, xhalf, xin), xfull, xin)
     arrived([p_last])
 
-    def set_block(rows_by_part):
-        top = as_rows(rows_by_part)
-        n = top.shape[1] // 2
-        bottom = jnp.concatenate([-top[:, n:], top[:, :n]], axis=1)
-        for i, (above, below) in enumerate(zip(halves(top), halves(bottom))):
+    def set_block(top):
+        n = top[0].shape[1] // 2
+        for i, above in enumerate(top):
             wt[i, :npiv] = above
-            wt[i, npiv:] = below
-        return top, bottom
+            wt[i, npiv:, :n] = -above[:, n:]
+            wt[i, npiv:, n:] = above[:, :n]
 
     to_row = lax.broadcasted_iota(jnp.int32, (emb, emb), 0)
     from_row = lax.broadcasted_iota(jnp.int32, (emb, emb), 1)
     by_part = (from_row == lax.rem(to_row, nx * ny) * 8 + to_row // (nx * ny)).astype(F32).astype(BF16)
     pivots = chosen(by_part, pall[...])
-    top, bottom = set_block(pivots)
-    gram = product((wt[0, :npiv], wt[1, :npiv]), halves(top + bottom), NT)
+    mixed = jnp.concatenate([pivots[:npiv] - pivots[npiv:], pivots[:npiv] + pivots[npiv:]], axis=1)
+    top = halves(as_rows(pivots))
+    gram = product(top, halves(mixed), NT)
     for i in range(nz * nc):
         gpart[i] = gram[i * gpart.shape[1] : (i + 1) * gpart.shape[1]]
     g_scatter = fan([(gpart.at[to[2] * nc + to[3]], gin.at[i], to) for i, to in fs], g_s.at[0], g_r.at[0], gin)
+    set_block(top)
     for d in order:
         k_forward(d)
     scatter_rows(cpart, product((live_h[0], live_h[1]), (wt[0], wt[1]), NT))
     c_pair = pair_up(1, cpart, cpair)
+    x_last = share(0, x_spread, xfull)
+    d_last = share(2, d_spread, dfull)
 
     c_scatter = scatter(1, c_pair, cpart, cpair, chalf, cin)
     arrived([g_scatter])
@@ -314,8 +339,8 @@
         total = total + gin[i]
     gfull[f] = total
     g_gather = fan([(gfull.at[f], gfull.at[f], to) for _, to in fs], g_s.at[1], g_r.at[1], gin)
-    x_last = share(0, x_spread, xfull)
-    arrived([x_last])
+    c_spread = spread(1, gathered(c_scatter, chalf, cin), cfull, cin)
+    arrived([x_last, d_last])
     arrived([k_last])
 
     inner = halves(xfull[...].reshape(nb, nb))
@@ -335,11 +360,9 @@
     _, k_both = split_rows(proj)
     t_rows, t_both = split_rows(taken)
     less = product(t_rows, k_both, NT) + product(rest, t_both, NT)
-    kept = gathered(d_scatter, dhalf, din)
-    total = gathered(c_scatter, chalf, cin)
-    c_spread = spread(1, total - product(halves(kept), t_both, NT), cfull, cin)
+    cross_less = product(halves(dfull[...].reshape(rows, 2 * nb)), t_both, NT)
     taken = halves(taken)
-    set_block(pivots - crossed(product(taken, b_re, NN), product(taken, b_im, NN)))
+    set_block(halves(as_rows(pivots - crossed(product(taken, b_re, NN), product(taken, b_im, NN)))))
     w = (wt[0], wt[1])
     arrived([g_gather])
 
@@ -375,7 +398,7 @@
 
     zed_e = tuple(embedded(part) for part in halves(zed))
     arrived([c_last])
-    cross = cfull[...].reshape(rows, emb)
+    cross = cfull[...].reshape(rows, emb) - cross_less
     coef = product(halves(cross * scale_row), zed_e, NT)
     coef_re[...] = coef[:, :npiv]
     coef_im[...] = coef[:, npiv:]
@@ -444,7 +467,9 @@
         vmem((1, rows), jnp.int32),
         vmem((1, emb // 2), jnp.int32),
         vmem((emb, bins), F32),
-        vmem((nx - 1, span, bins), F32),
+        vmem((2, span, bins // 2), F32),
+        vmem((2, span, bins // 2), F32),
+        vmem((2, span, bins), F32),
         vmem((span, bins), F32),
         vmem((ny - 1, 8, bins), F32),
         vmem((8, nb), F32),
@@ -457,12 +482,12 @@
         *[vmem((count, emb // 2 // nf, emb // 2), F32) for count in (nf, nf - 1, nf)],
         vmem(((nx - 1) * ny, 8, nb), F32),
         *summed(rows, emb),
-        *summed(rows, 2 * nb)[:4],
+        *summed(rows, 2 * nb),
         vmem((1, rows), F32), vmem((nf, 1, rows), F32),
         dma((6,)),
-        *[dma((1,))] * 6, *[dma((3,))] * 2,
+        *[dma((2, 2))] * 2, *[dma((1,))] * 2, *[dma((2, 2))] * 2, *[dma((1,))] * 4, *[dma((3,))] * 2,
         *[dma((1,)), dma((ny - 1,)), dma((1,)), dma((1,))] * 2,
-        *[dma((3,))] * 2, *[dma((2,))] * 2, *[dma((2,))] * 2, *[dma((2,))] * 2, *[dma((1,))] * 2,
+        *[dma((3,))] * 6, *[dma((2,))] * 2, *[dma((1,))] * 2,
         dma((5,)),
     ]
     here = pl.BlockSpec(memory_space=pltpu.VMEM)

time: 65 us -> 64.1 us (0.986)
  Pallas kernels: 64.3 us -> 63.3 us
    pallas_call x1, Pallas kernels: 63.2 us -> 62.2 us  [body(): pl.pallas_call(functools.partial(kernel, torus), out_shape=[vmem(shape, F...]
where the time goes in v6:
time: 64.1 us; the launch traced here: 64 us
  Pallas kernels  63.3 us (99%)
    pallas_call x1, Pallas kernels, body(): pl.pallas_call(functools.partial(kernel, torus), out_shape=[vmem(shape, F...  62.2 us

profile of v6, /device:TPU:1, one launch (start us, length us, event | category | flops | bytes accessed | tf_op | source)
XLA Modules:
  0.0 64.0 jit_solution(488878422719035733)
XLA Ops:
  0.6 62.2 %shard_map.101 = (f32[256,128]{1,0:T(8,128)S(1)}, f32[256,128]{1,0:T(8,128)S(1)}, f32[256,512]{1,0:T(8,128)S(1)}, f32[256,512]{1,0:T(8,128)S(1)}, f32[1,256]{1,0:T(1,128)S(1)}) custom-call(f32[256,512]{1,0:T(8,128)} %res_re.1, f32[256,512]{1,0:T(8,128)} %res_im.1, f32[256,512]{1,0:T(8,128)} %basis_re.1, f32[256,512]{1,0:T(8,128)} %basis_im.1, ...), custom_call_target="tpu_custom_call" | custom-call | tf_op jit(solution)/shard_map/pallas_call | solution.py:495
  62.9 1.1 %shard_map.102 = (f32[256,128]{1,0:T(8,128)}, f32[256,128]{1,0:T(8,128)}, f32[256,512]{1,0:T(8,128)}, f32[256,512]{1,0:T(8,128)}, f32[1,256]{1,0:T(1,128)}) custom-call(f32[256,128]{1,0:T(8,128)S(1)} %get-tuple-element.15.refs_0_, f32[256,128]{1,0:T(8,128)S(1)} %get-tuple-element.16.refs_1_, f32[256,512]{1,0:T(8,128)S(1)} %get-tuple-element.17.refs_2_, ...), custom_call_target="tpu_custom_call" | custom-call | tf_op jit(solution)/shard_map/pallas_call | solution.py:503

commit v7 on v6

--- a/solution.py
+++ b/solution.py
@@ -295,10 +295,10 @@
     a, b = short_product(chunk, (b_re, b_im), NT)
     kout[...] = a + sign_k * pltpu.roll(b, 4, 0)
     k_copies = fan([(kout, kin.at[i], to) for i, to in fs], k_s.at[0], k_r.at[0], kin)
+    x_spread = spread(0, gathered(x_scatter, xhalf, xin), xfull, xin)
+    d_spread = spread(2, gathered(d_scatter, dhalf, din), dfull, din)
     for d in order:
         p_forward(d)
-    x_spread = spread(0, gathered(x_scatter, xhalf, xin), xfull, xin)
-    d_spread = spread(2, gathered(d_scatter, dhalf, din), dfull, din)
     arrived([k_copies])
     proj = kout[...]
     for i in range(len(fs)):
@@ -317,22 +317,26 @@
     to_row = lax.broadcasted_iota(jnp.int32, (emb, emb), 0)
     from_row = lax.broadcasted_iota(jnp.int32, (emb, emb), 1)
     by_part = (from_row == lax.rem(to_row, nx * ny) * 8 + to_row // (nx * ny)).astype(F32).astype(BF16)
-    pivots = chosen(by_part, pall[...])
+
+    def by_parts(a):
+        return tuple(dot(by_part, part, NN).astype(BF16) for part in halves(a))
+
+    pivot_halves = by_parts(pall[...])
+    pivots = pivot_halves[0].astype(F32) + pivot_halves[1].astype(F32)
     mixed = jnp.concatenate([pivots[:npiv] - pivots[npiv:], pivots[:npiv] + pivots[npiv:]], axis=1)
-    top = halves(as_rows(pivots))
+    top = tuple(as_rows(part) for part in pivot_halves)
     gram = product(top, halves(mixed), NT)
     for i in range(nz * nc):
         gpart[i] = gram[i * gpart.shape[1] : (i + 1) * gpart.shape[1]]
     g_scatter = fan([(gpart.at[to[2] * nc + to[3]], gin.at[i], to) for i, to in fs], g_s.at[0], g_r.at[0], gin)
     set_block(top)
+    scatter_rows(cpart, product((live_h[0], live_h[1]), (wt[0], wt[1]), NT))
+    c_pair = pair_up(1, cpart, cpair)
+    c_scatter = scatter(1, c_pair, cpart, cpair, chalf, cin)
     for d in order:
         k_forward(d)
-    scatter_rows(cpart, product((live_h[0], live_h[1]), (wt[0], wt[1]), NT))
-    c_pair = pair_up(1, cpart, cpair)
     x_last = share(0, x_spread, xfull)
     d_last = share(2, d_spread, dfull)
-
-    c_scatter = scatter(1, c_pair, cpart, cpair, chalf, cin)
     arrived([g_scatter])
     total = gpart[f]
     for i in range(len(fs)):
@@ -345,23 +349,21 @@
 
     inner = halves(xfull[...].reshape(nb, nb))
 
-    def times_inner(a):
-        both = halves(a)
+    def times_inner(both):
         straight, across = product(both, inner, NN), product(both, inner, NT)
         return crossed(0.5 * (straight + across), 0.5 * (straight - across))
 
-    def split_rows(a):
-        parts = halves(as_rows(a))
-        return parts, tuple(embedded(part) for part in parts)
-
-    proj = chosen(by_part, kall[...])
-    taken = 2.0 * proj - times_inner(proj)
-    rest, _ = split_rows(proj - times_inner(taken))
-    _, k_both = split_rows(proj)
-    t_rows, t_both = split_rows(taken)
+    proj_halves = by_parts(kall[...])
+    proj = proj_halves[0].astype(F32) + proj_halves[1].astype(F32)
+    taken = 2.0 * proj - times_inner(proj_halves)
+    taken_halves = halves(taken)
+    rest = halves(as_rows(proj - times_inner(taken_halves)))
+    k_both = tuple(embedded(as_rows(part)) for part in proj_halves)
+    t_rows = tuple(as_rows(part) for part in taken_halves)
+    t_both = tuple(embedded(part) for part in t_rows)
     less = product(t_rows, k_both, NT) + product(rest, t_both, NT)
     cross_less = product(halves(dfull[...].reshape(rows, 2 * nb)), t_both, NT)
-    taken = halves(taken)
+    taken = taken_halves
     set_block(halves(as_rows(pivots - crossed(product(taken, b_re, NN), product(taken, b_im, NN)))))
     w = (wt[0], wt[1])
     arrived([g_gather])

time: 64.1 us -> 62 us (0.967)
  Pallas kernels: 63.3 us -> 61.2 us
    pallas_call x1, Pallas kernels: 62.2 us -> 60.1 us  [body(): pl.pallas_call(functools.partial(kernel, torus), out_shape=[vmem(shape, F...]
where the time goes in v7:
time: 62 us; the launch traced here: 61.9 us
  Pallas kernels  61.2 us (99%)
  between operations  0.64 us (1%)
    pallas_call x1, Pallas kernels, body(): pl.pallas_call(functools.partial(kernel, torus), out_shape=[vmem(shape, F...  60.1 us

profile of v7, /device:TPU:1, one launch (start us, length us, event | category | flops | bytes accessed | tf_op | source)
XLA Modules:
  0.0 61.9 jit_solution(3626409098819758123)
XLA Ops:
  0.6 60.1 %shard_map.101 = (f32[256,128]{1,0:T(8,128)S(1)}, f32[256,128]{1,0:T(8,128)S(1)}, f32[256,512]{1,0:T(8,128)S(1)}, f32[256,512]{1,0:T(8,128)S(1)}, f32[1,256]{1,0:T(1,128)S(1)}) custom-call(f32[256,512]{1,0:T(8,128)} %res_re.1, f32[256,512]{1,0:T(8,128)} %res_im.1, f32[256,512]{1,0:T(8,128)} %basis_re.1, f32[256,512]{1,0:T(8,128)} %basis_im.1, ...), custom_call_target="tpu_custom_call" | custom-call | tf_op jit(solution)/shard_map/pallas_call | solution.py:497
  60.8 1.1 %shard_map.102 = (f32[256,128]{1,0:T(8,128)}, f32[256,128]{1,0:T(8,128)}, f32[256,512]{1,0:T(8,128)}, f32[256,512]{1,0:T(8,128)}, f32[1,256]{1,0:T(1,128)}) custom-call(f32[256,128]{1,0:T(8,128)S(1)} %get-tuple-element.15.refs_0_, f32[256,128]{1,0:T(8,128)S(1)} %get-tuple-element.16.refs_1_, f32[256,512]{1,0:T(8,128)S(1)} %get-tuple-element.17.refs_2_, ...), custom_call_target="tpu_custom_call" | custom-call | tf_op jit(solution)/shard_map/pallas_call | solution.py:505

commit v8 on v7

--- a/solution.py
+++ b/solution.py
@@ -37,11 +37,19 @@
     return high, mid, (rest - mid.astype(F32)).astype(BF16)
 
 
-def product(left, right, dims):
+def joined(left, right, dims):
     lh, ll = left
     rh, rl = right
     along = dims[1][0]
     return dot(jnp.concatenate([lh, ll, lh], axis=1), jnp.concatenate([rh, rh, rl], axis=along), dims)
+
+
+def product(left, right, dims):
+    lh, ll = left
+    rh, rl = right
+    rows = lh.shape[0]
+    both = dot(jnp.concatenate([lh, ll], axis=0), rh, dims)
+    return both[:rows] + (both[rows:] + dot(lh, rl, dims))
 
 
 def chosen(select, a):
@@ -83,8 +91,8 @@
     coef_re, coef_im, new_re, new_im, err,
     xpart, xpair, xhalf, xin, xfull, gpart, gin, gfull, kspan,
     cpart, cpair, chalf, cin, cfull, dpart, dpair, dhalf, din, dfull, eout, ein,
-    in_s, rf_s, rf_r, rn_s, rn_r, rr_s, rr_r, ry_s, ry_r, k_s, k_r, p_s, p_r, py_s, py_r, px_s, px_r, ky_s, ky_r, kx_s, kx_r,
-    zs_s, zs_r, zg_s, zg_r, c_s, c_r, g_s, g_r, e_s, e_r, out_s,
+    in_s, rf_s, rf_r, rn_s, rn_r, ry_s, ry_r, k_s, k_r, p_s, p_r, py_s, py_r, px_s, px_r, ky_s, ky_r, kx_s, kx_r,
+    zs_s, zs_r, zg_s, zg_r, cz_r, c_s, c_r, g_s, g_r, e_s, e_r, out_s,
 ):
     nx, ny, nz, nc = torus
     x, y, z, c = (lax.axis_index(a) for a in AXES)
@@ -170,7 +178,10 @@
     own = (x * ny + y) * rows + lax.broadcasted_iota(jnp.int32, (emb, rows), 1)
     select = (wanted == own.astype(F32)).astype(F32).astype(BF16)
     is_im = lax.rem(lax.broadcasted_iota(jnp.int32, (emb, bins), 0), 8) // 4
-    picked[...] = jnp.where(is_im == 0, chosen(select, live[:, :bins]), chosen(select, live[:, bins:]))
+    for i, value in enumerate(halves(live[...])):
+        live_h[i] = value
+    both = sum(dot(select, live_h[i], NN) for i in range(2))
+    picked[...] = jnp.where(is_im == 0, both[:, :bins], both[:, bins:])
 
     pl.semaphore_wait(barrier, len(peers))
 
@@ -183,11 +194,9 @@
         for k, (to, _, lanes) in enumerate(ways):
             at = pl.ds(pl.multiple_of(across * span + i * piece, piece), piece)
             far_copies.append(
-                push(picked.at[at, lanes], far.at[k, pl.ds(i * piece, piece)], rf_s.at[i, k], rf_r.at[i, k], to)
+                begin(picked.at[at, lanes], far.at[k, pl.ds(i * piece, piece)], rf_s.at[0], rf_r.at[i, k], to)
             )
 
-    for i, value in enumerate(halves(live[...])):
-        live_h[i] = value
     for load in loads[4:]:
         load.wait()
     for i in range(2):
@@ -198,7 +207,7 @@
     b_im = (base[2], base[3])
     plus = jnp.concatenate([basis[0] + basis[1], basis[1] - basis[0]], axis=1)
     right_side = tuple(jnp.concatenate([base[i], base[2 + i]], axis=1) for i in range(2))
-    both = product(halves(plus), right_side, NT)
+    both = joined(halves(plus), right_side, NT)
 
     def scatter_rows(part, value):
         size = part.shape[2]
@@ -235,16 +244,18 @@
         (picked.at[chunk_of(next_x, span), other], near.at[k, :, other], to)
         for k, ((to, next_x, _), other) in enumerate(zip(ways, (behind, ahead)))
     ]
-    near_begun = fan(near_started, rn_s.at[0], rn_r.at[0], far)
+    for src, dst, to in near_started:
+        begin(src, dst, rn_s.at[0], rn_r.at[0], to)
+    near_begun = described(near, near, rn_s.at[0], rn_r.at[0], anyone)
+    finals.append(near_begun)
     scatter_rows(xpart, both)
     x_pair = pair_up(0, xpart, xpair)
     turned_side = tuple(jnp.concatenate([-base[2 + i], base[i]], axis=1) for i in range(2))
     both = tuple(jnp.concatenate([right_side[i], turned_side[i]], axis=0) for i in range(2))
-    scatter_rows(dpart, product((live_h[0], live_h[1]), both, NT))
+    scatter_rows(dpart, joined((live_h[0], live_h[1]), both, NT))
     x_scatter = scatter(0, x_pair, xpart, xpair, xhalf, xin)
     d_pair = pair_up(2, dpart, dpair)
 
-    relays = []
     for i in range(2):
         for k, (to, next_x, lanes) in enumerate(ways):
             arrived([far_copies[2 * i + k]])
@@ -253,9 +264,10 @@
             relay[k, i * piece : (i + 1) * piece] = (
                 picked[at, k * half : (k + 1) * half] + far[k, i * piece : (i + 1) * piece]
             )
-            relays.append(push(relay.at[k, part], near.at[k, part, lanes], rr_s.at[i, k], rr_r.at[i, k], to))
+            begin(relay.at[k, part], near.at[k, part, lanes], rn_s.at[0], rn_r.at[0], to)
+    finals.append(described(far, far, rf_s.at[0], rf_r.at[0, 0], anyone))
     d_scatter = scatter(2, d_pair, dpart, dpair, dhalf, din)
-    arrived([near_begun, *relays])
+    arrived([near_begun])
     ysum[...] = picked[chunk_of(x, span), :] + near[0] + near[1]
     y_copies = fan([(ysum.at[chunk_of(p, 8)], yr.at[i], (x, p, z, c)) for i, p in ys], ry_s.at[0], ry_r.at[0], yr)
     arrived([y_copies])
@@ -343,7 +355,12 @@
         total = total + gin[i]
     gfull[f] = total
     g_gather = fan([(gfull.at[f], gfull.at[f], to) for _, to in fs], g_s.at[1], g_r.at[1], gin)
-    c_spread = spread(1, gathered(c_scatter, chalf, cin), cfull, cin)
+    cfull[c, z] = gathered(c_scatter, chalf, cin)
+    c_own = cfull.at[c, z]
+    c_spread = {i: begin(c_own, c_own, zg_s.at[1], cz_r.at[i], (x, y, p, c)) for i, p in zs}
+    begin(c_own, c_own, c_s.at[1], c_r.at[1], (x, y, z, 1 - c))
+    c_last = described(cfull.at[c], cfull.at[c], c_s.at[1], c_r.at[1], anyone)
+    finals.extend([described(cin, cin, zg_s.at[1], zg_r.at[1], anyone), c_last])
     arrived([x_last, d_last])
     arrived([k_last])
 
@@ -386,8 +403,11 @@
         return product(left, tuple(embedded(part) for part in right), NN)
 
     for step in range(NS_STEPS):
-        if step == 3:
-            c_last = share(1, c_spread, cfull)
+        if step == NS_STEPS - 1:
+            for i in sorted(range(nz - 1), key=lambda i: hops(i + 1, nz)):
+                arrived([c_spread[i]])
+                theirs = cfull.at[c, lax.rem(z + nz - 1 - i, nz)]
+                begin(theirs, theirs, c_s.at[1], c_r.at[1], (x, y, z, 1 - c))
         yh = halves(your)
         mix = your if zed is None else times(zh, yh)
         s = 1.5 * ident - 0.5 * mix
@@ -487,9 +507,9 @@
         *summed(rows, 2 * nb),
         vmem((1, rows), F32), vmem((nf, 1, rows), F32),
         dma((6,)),
-        *[dma((2, 2))] * 2, *[dma((1,))] * 2, *[dma((2, 2))] * 2, *[dma((1,))] * 4, *[dma((3,))] * 2,
+        dma((1,)), dma((2, 2)), *[dma((1,))] * 6, *[dma((3,))] * 2,
         *[dma((1,)), dma((ny - 1,)), dma((1,)), dma((1,))] * 2,
-        *[dma((3,))] * 6, *[dma((2,))] * 2, *[dma((1,))] * 2,
+        *[dma((3,))] * 4, dma((nz - 1,)), *[dma((3,))] * 2, *[dma((2,))] * 2, *[dma((1,))] * 2,
         dma((5,)),
     ]
     here = pl.BlockSpec(memory_space=pltpu.VMEM)

time: 62 us -> 61.2 us (0.987)
  Pallas kernels: 61.2 us -> 60.5 us
    pallas_call x1, Pallas kernels: 60.1 us -> 59.4 us  [body(): pl.pallas_call(functools.partial(kernel, torus), out_shape=[vmem(shape, F...]
where the time goes in v8:
time: 61.2 us; the launch traced here: 61.1 us
  Pallas kernels  60.5 us (99%)
  between operations  0.64 us (1%)
    pallas_call x1, Pallas kernels, body(): pl.pallas_call(functools.partial(kernel, torus), out_shape=[vmem(shape, F...  59.4 us

profile of v8, /device:TPU:1, one launch (start us, length us, event | category | flops | bytes accessed | tf_op | source)
XLA Modules:
  0.0 61.1 jit_solution(8475620118163043435)
XLA Ops:
  0.6 59.4 %shard_map.101 = (f32[256,128]{1,0:T(8,128)S(1)}, f32[256,128]{1,0:T(8,128)S(1)}, f32[256,512]{1,0:T(8,128)S(1)}, f32[256,512]{1,0:T(8,128)S(1)}, f32[1,256]{1,0:T(1,128)S(1)}) custom-call(f32[256,512]{1,0:T(8,128)} %res_re.1, f32[256,512]{1,0:T(8,128)} %res_im.1, f32[256,512]{1,0:T(8,128)} %basis_re.1, f32[256,512]{1,0:T(8,128)} %basis_im.1, ...), custom_call_target="tpu_custom_call" | custom-call | tf_op jit(solution)/shard_map/pallas_call | solution.py:517
  60.0 1.1 %shard_map.102 = (f32[256,128]{1,0:T(8,128)}, f32[256,128]{1,0:T(8,128)}, f32[256,512]{1,0:T(8,128)}, f32[256,512]{1,0:T(8,128)}, f32[1,256]{1,0:T(1,128)}) custom-call(f32[256,128]{1,0:T(8,128)S(1)} %get-tuple-element.15.refs_0_, f32[256,128]{1,0:T(8,128)S(1)} %get-tuple-element.16.refs_1_, f32[256,512]{1,0:T(8,128)S(1)} %get-tuple-element.17.refs_2_, ...), custom_call_target="tpu_custom_call" | custom-call | tf_op jit(solution)/shard_map/pallas_call | solution.py:525

commit v9 on v8

--- a/solution.py
+++ b/solution.py
@@ -112,7 +112,9 @@
     fs = sorted(((dz, dc) for dz in range(nz) for dc in range(nc) if dz or dc), key=lambda d: -hops(d[0], nz))
     fs = [(dz * nc + dc - 1, (x, y, lax.rem(z + dz, nz), lax.rem(c + dc, nc))) for dz, dc in fs]
     barrier = pltpu.get_barrier_semaphore()
-    peers = [to for _, to in fs] + [(x, p, z, c) for _, p in ys] + [(p, y, z, c) for _, p in xs]
+    peers = [(hops(i + 1, ny), (x, p, z, c)) for i, p in ys] + [(hops(i + 1, nx), (p, y, z, c)) for i, p in xs]
+    peers += [(hops((i + 1) // nc, nz), to) for i, to in fs]
+    peers = [to for _, to in sorted(peers, key=lambda peer: -peer[0])]
     for peer in peers:
         pl.semaphore_signal(barrier, inc=1, device_id=peer, device_id_type=pl.DeviceIdType.MESH)
     loads = [(lens, vlen), (piv, vpiv), (res_re, live.at[:, pl.ds(0, bins)]), (res_im, live.at[:, pl.ds(bins, bins)])]
@@ -185,12 +187,13 @@
 
     pl.semaphore_wait(barrier, len(peers))
 
-    half, piece = bins // 2, span // 2
+    half, pieces = bins // 2, 4
+    piece = span // pieces
     ahead, behind = pl.ds(0, half), pl.ds(half, half)
     right, left, across = (lax.rem(x + d, nx) for d in (1, nx - 1, 2))
     ways = (((right, y, z, c), right, ahead), ((left, y, z, c), left, behind))
     far_copies = []
-    for i in range(2):
+    for i in range(pieces):
         for k, (to, _, lanes) in enumerate(ways):
             at = pl.ds(pl.multiple_of(across * span + i * piece, piece), piece)
             far_copies.append(
@@ -256,7 +259,7 @@
     x_scatter = scatter(0, x_pair, xpart, xpair, xhalf, xin)
     d_pair = pair_up(2, dpart, dpair)
 
-    for i in range(2):
+    for i in range(pieces):
         for k, (to, next_x, lanes) in enumerate(ways):
             arrived([far_copies[2 * i + k]])
             at = pl.ds(pl.multiple_of(next_x * span + i * piece, piece), piece)
@@ -507,7 +510,7 @@
         *summed(rows, 2 * nb),
         vmem((1, rows), F32), vmem((nf, 1, rows), F32),
         dma((6,)),
-        dma((1,)), dma((2, 2)), *[dma((1,))] * 6, *[dma((3,))] * 2,
+        dma((1,)), dma((4, 2)), *[dma((1,))] * 6, *[dma((3,))] * 2,
         *[dma((1,)), dma((ny - 1,)), dma((1,)), dma((1,))] * 2,
         *[dma((3,))] * 4, dma((nz - 1,)), *[dma((3,))] * 2, *[dma((2,))] * 2, *[dma((1,))] * 2,
         dma((5,)),

time: 61.2 us -> 60.8 us (level)
  no operation moved by 1% of the time
where the time goes in v9:
time: 60.8 us; the launch traced here: 60.7 us
  Pallas kernels  60 us (99%)
  between operations  0.64 us (1%)
    pallas_call x1, Pallas kernels, body(): pl.pallas_call(functools.partial(kernel, torus), out_shape=[vmem(shape, F...  58.9 us

profile of v9, /device:TPU:1, one launch (start us, length us, event | category | flops | bytes accessed | tf_op | source)
XLA Modules:
  0.0 60.7 jit_solution(10990121157210529464)
XLA Ops:
  0.6 58.9 %shard_map.101 = (f32[256,128]{1,0:T(8,128)S(1)}, f32[256,128]{1,0:T(8,128)S(1)}, f32[256,512]{1,0:T(8,128)S(1)}, f32[256,512]{1,0:T(8,128)S(1)}, f32[1,256]{1,0:T(1,128)S(1)}) custom-call(f32[256,512]{1,0:T(8,128)} %res_re.1, f32[256,512]{1,0:T(8,128)} %res_im.1, f32[256,512]{1,0:T(8,128)} %basis_re.1, f32[256,512]{1,0:T(8,128)} %basis_im.1, ...), custom_call_target="tpu_custom_call" | custom-call | tf_op jit(solution)/shard_map/pallas_call | solution.py:520
  59.6 1.1 %shard_map.102 = (f32[256,128]{1,0:T(8,128)}, f32[256,128]{1,0:T(8,128)}, f32[256,512]{1,0:T(8,128)}, f32[256,512]{1,0:T(8,128)}, f32[1,256]{1,0:T(1,128)}) custom-call(f32[256,128]{1,0:T(8,128)S(1)} %get-tuple-element.15.refs_0_, f32[256,128]{1,0:T(8,128)S(1)} %get-tuple-element.16.refs_1_, f32[256,512]{1,0:T(8,128)S(1)} %get-tuple-element.17.refs_2_, ...), custom_call_target="tpu_custom_call" | custom-call | tf_op jit(solution)/shard_map/pallas_call | solution.py:528

commit v10 on v9

--- a/solution.py
+++ b/solution.py
@@ -310,9 +310,11 @@
     a, b = short_product(chunk, (b_re, b_im), NT)
     kout[...] = a + sign_k * pltpu.roll(b, 4, 0)
     k_copies = fan([(kout, kin.at[i], to) for i, to in fs], k_s.at[0], k_r.at[0], kin)
+    for d in order[:4]:
+        p_forward(d)
     x_spread = spread(0, gathered(x_scatter, xhalf, xin), xfull, xin)
     d_spread = spread(2, gathered(d_scatter, dhalf, din), dfull, din)
-    for d in order:
+    for d in order[4:]:
         p_forward(d)
     arrived([k_copies])
     proj = kout[...]

time: 60.8 us -> 60.9 us (level)
  no operation moved by 1% of the time
where the time goes in v10:
time: 60.9 us; the launch traced here: 60.7 us
  Pallas kernels  60.1 us (99%)
  between operations  0.64 us (1%)
    pallas_call x1, Pallas kernels, body(): pl.pallas_call(functools.partial(kernel, torus), out_shape=[vmem(shape, F...  59 us

profile of v10, /device:TPU:1, one launch (start us, length us, event | category | flops | bytes accessed | tf_op | source)
XLA Modules:
  0.0 60.7 jit_solution(11214930702294864668)
XLA Ops:
  0.6 59.0 %shard_map.101 = (f32[256,128]{1,0:T(8,128)S(1)}, f32[256,128]{1,0:T(8,128)S(1)}, f32[256,512]{1,0:T(8,128)S(1)}, f32[256,512]{1,0:T(8,128)S(1)}, f32[1,256]{1,0:T(1,128)S(1)}) custom-call(f32[256,512]{1,0:T(8,128)} %res_re.1, f32[256,512]{1,0:T(8,128)} %res_im.1, f32[256,512]{1,0:T(8,128)} %basis_re.1, f32[256,512]{1,0:T(8,128)} %basis_im.1, ...), custom_call_target="tpu_custom_call" | custom-call | tf_op jit(solution)/shard_map/pallas_call | solution.py:522
  59.6 1.1 %shard_map.102 = (f32[256,128]{1,0:T(8,128)}, f32[256,128]{1,0:T(8,128)}, f32[256,512]{1,0:T(8,128)}, f32[256,512]{1,0:T(8,128)}, f32[1,256]{1,0:T(1,128)}) custom-call(f32[256,128]{1,0:T(8,128)S(1)} %get-tuple-element.15.refs_0_, f32[256,128]{1,0:T(8,128)S(1)} %get-tuple-element.16.refs_1_, f32[256,512]{1,0:T(8,128)S(1)} %get-tuple-element.17.refs_2_, ...), custom_call_target="tpu_custom_call" | custom-call | tf_op jit(solution)/shard_map/pallas_call | solution.py:530
